TPU v7x, 256 devices: a whole 4x4x8 slice. The times are simulated.
256 devices in a mesh: expert: 32 (over y, x, core), dp: 8 (over z).
Axes of the slice: x: 4, y: 4, z: 8, core: 2. Of those that a mesh axis runs over, the one named last changes fastest.
Arguments:
- tokens: bfloat16 [32768, 2048], P(('expert', 'dp')), may hold values from -6 to 6
- cotangent: bfloat16 [32768, 2048], P(('expert', 'dp')), may hold values from -6 to 6
- gate_weights: float32 [32768, 8], P(('expert', 'dp')), may hold values from 0.02 to 0.5
- expert_ids: int32 [32768, 8], P(('expert', 'dp')), may hold values from 0 to 63, as said below
- copy_pick: int32 [32768, 8], P(('expert', 'dp')), may hold values from 0 to 1, as said below
- copy_expert: int32 [32], replicated, may hold values from 0 to 63, as said below
- up_weight: bfloat16 [64, 2048, 384], P('expert'), may hold values from -0.125 to 0.125
- down_weight: bfloat16 [64, 384, 2048], P('expert'), may hold values from -0.3125 to 0.3125
- copy_up: bfloat16 [32, 2048, 384], P('expert'), may hold values from -0.125 to 0.125
- copy_down: bfloat16 [32, 384, 2048], P('expert'), may hold values from -0.3125 to 0.3125
Outputs:
- layer_output: bfloat16 [32768, 2048], P(('expert', 'dp'))
- token_grad: bfloat16 [32768, 2048], P(('expert', 'dp'))
- gate_grad: float32 [32768, 8], P(('expert', 'dp'))
- up_grad: bfloat16 [64, 2048, 384], P('expert', 'dp')
- down_grad: bfloat16 [64, 384, 2048], P('expert', None, 'dp')
Inputs may be any that keep to these rules, and one draw needn't show every extreme that they name: `expert_ids`: each row names 8 different experts. In the 128 rows of one device, the 2 experts of any one device are named 8 * 128 // 32 times together; the one of them that copy_expert lists is named at most 16 + 8 times and the other at most 16 - 8 + 8 // 2 times, and both bounds are reached in every block of rows. `copy_pick`: A 1 stands only where the pair's expert is listed in copy_expert. From the rows of one device at most 6 pairs go to one copy and at most 38 pairs go to one device (its own experts and its copy together). In each group of devices that share an index along dp, some device receives exactly 38 pairs from every device of the group, and the copy before it exactly 6 from each. `copy_expert`: entry c is one of the experts of device c - 1 along the expert axis (of the last device for entry 0); device o holds the experts 2 * o to 2 * o + 1.
All inputs are finite; a program needn't handle non-finite values.
Results may differ from a plain program's by a relative error of at most 0.014.
Values may be sent and summed in bfloat16 or wider, within the bound.
A program may use at most 128 MiB of HBM per device.

v0:
```python
import functools

import jax
import jax.numpy as jnp
from jax import lax
from jax.experimental import pallas as pl
from jax.experimental.pallas import tpu as pltpu
from jax.sharding import PartitionSpec as P

SIDE = 4
HOT, COLD, COPY = 24, 12, 6
SLOTS = 48
REPLICAS = 8
DEVICES = 2 * SIDE * SIDE
HOT_U, COLD_U, COPY_U = SIDE * HOT, SIDE * COLD, 32
UNIT = HOT_U + COLD_U + COPY_U
SPANS = ((0, HOT_U), (HOT_U, COLD_U), (HOT_U + COLD_U, COPY_U))
BF = jnp.bfloat16
F32 = jnp.float32
EXACT = lax.Precision.HIGHEST


def iota(shape, dim):
    return lax.broadcasted_iota(jnp.int32, shape, dim)


def route_kernel(ids_ref, picks_ref, gates_ref, listed_ref, table_ref, dest_ref, slot_ref):
    chosen, rows = ids_ref.shape
    ids, picks, gates = ids_ref[...], picks_ref[...], gates_ref[...]
    listed = listed_ref[...]
    devices = listed.shape[0]
    before = (iota((rows, rows), 0) < iota((rows, rows), 1)).astype(BF)
    lines = iota((128, rows), 0)
    token = iota((128, rows), 1).astype(F32) + 1.0
    offset = jnp.zeros((128, 1), F32)
    table = jnp.zeros((devices, 128), F32)
    for k in range(chosen):
        e, p, g = ids[k : k + 1], picks[k : k + 1], gates[k : k + 1]
        hot = jnp.max((e == listed).astype(jnp.int32), axis=0, keepdims=True)
        dest = (e // 2 + p) % devices
        region = jnp.where(p == 1, 2, 1 - hot)
        hit = (region * devices + dest == lines).astype(F32)
        ahead = jnp.dot(hit.astype(BF), before, preferred_element_type=F32) + offset
        rank = jnp.sum(hit * ahead, axis=0, keepdims=True).astype(jnp.int32)
        offset = offset + jnp.sum(hit, axis=1, keepdims=True)
        base = jnp.where(region == 0, 0, jnp.where(region == 1, HOT, HOT + COLD))
        slot = base + rank
        to = (dest == iota((devices, rows), 0)).astype(F32)
        value = jnp.where(slot == lines, token, 0.0) + jnp.where(slot + 64 == lines, g, 0.0)
        table = table + across(to, value, EXACT)
        dest_ref[k : k + 1] = dest
        slot_ref[k : k + 1] = slot
    table_ref[...] = table


def across(a, b, precision=None):
    return lax.dot_general(
        a, b, (((1,), (1,)), ((), ())), precision=precision, preferred_element_type=F32
    )


def route(ids, picks, gates, listed):
    chosen, rows = ids.shape
    vmem = pl.BlockSpec(memory_space=pltpu.VMEM)
    return pl.pallas_call(
        route_kernel,
        out_shape=(
            jax.ShapeDtypeStruct((listed.shape[0], 128), F32),
            jax.ShapeDtypeStruct((chosen, rows), jnp.int32),
            jax.ShapeDtypeStruct((chosen, rows), jnp.int32),
        ),
        in_specs=[vmem] * 4,
        out_specs=(vmem,) * 3,
        name="route",
    )(ids, picks, gates, listed.reshape(-1, 1))


def gate_kernel(dest_ref, slot_ref, back_ref, out_ref):
    chosen, rows = dest_ref.shape
    devices = back_ref.shape[0]
    back = jnp.transpose(back_ref[...])
    for k in range(chosen):
        to = (dest_ref[k : k + 1] == iota((devices, rows), 0)).astype(F32)
        picked = jnp.dot(back, to, precision=EXACT, preferred_element_type=F32)
        mine = jnp.where(slot_ref[k : k + 1] == iota((128, rows), 0), picked, 0.0)
        out_ref[k : k + 1] = jnp.sum(mine, axis=0, keepdims=True)


def gate_back(dest, slot, back):
    vmem = pl.BlockSpec(memory_space=pltpu.VMEM)
    return pl.pallas_call(
        gate_kernel,
        out_shape=jax.ShapeDtypeStruct(dest.shape, F32),
        in_specs=[vmem] * 3,
        out_specs=vmem,
        name="gate_back",
    )(dest, slot, back)


def serve_kernel(
    which_ref, hot_t, cold_t, copy_t, hot_c, cold_c, copy_c, gates_ref, up_ref, down_ref,
    copy_up_ref, copy_down_ref, hot_o, cold_o, copy_o, hot_g, cold_g, copy_g, grads_ref, back_ref,
    x, c, u, v, o, q, w, linear, slope, active, sums, in_sem, out_sem,
):
    firsts = (0, hot_t.shape[0], hot_t.shape[0] + cold_t.shape[0])
    counts = (hot_t.shape[0], cold_t.shape[0], copy_t.shape[0])
    width = x.shape[1]
    step = 512
    hot = which_ref[0]
    ups = (up_ref.at[hot], up_ref.at[1 - hot], copy_up_ref.at[0])
    downs = (down_ref.at[hot], down_ref.at[1 - hot], copy_down_ref.at[0])

    def loads(r):
        span = pl.ds(firsts[r], counts[r])
        pairs = (
            ((hot_t, cold_t, copy_t)[r], x.at[span]),
            (ups[r], u.at[r]),
            (downs[r], v.at[r]),
            ((hot_c, cold_c, copy_c)[r], c.at[span]),
        )
        return [pltpu.make_async_copy(*pair, in_sem.at[r, i]) for i, pair in enumerate(pairs)]

    stores = []

    def store(src, dst, r, i):
        copy = pltpu.make_async_copy(src, dst, out_sem.at[r, i])
        copy.start()
        stores.append(copy)

    for r in (2, 1, 0):
        for copy in loads(r):
            copy.start()
    for r in (2, 1, 0):
        first, count = firsts[r], counts[r]
        span = pl.ds(first, count)
        ready = loads(r)
        gate = jnp.transpose(jnp.broadcast_to(gates_ref[:, first : first + count], (128, count)))
        gate = gate[:, :1]
        ready[0].wait()
        ready[1].wait()
        tile = min(count, 384)

        @pl.loop(0, count // tile)
        def _(i):
            rows = pl.ds(pl.multiple_of(i * tile, tile), tile)
            value = jnp.dot(
                x[pl.ds(pl.multiple_of(first + i * tile, 128), tile)], u[r],
                preferred_element_type=F32)
            sigma = 1.0 / (1.0 + jnp.exp(-value))
            slope[rows] = sigma * (1.0 + value * (1.0 - sigma))
            active[rows] = (value * sigma).astype(BF)
            linear[rows] = value * sigma

        sums[pl.ds(0, count)] = jnp.zeros((count, 128), F32)
        ready[2].wait()
        ready[3].wait()

        @pl.loop(0, width // step)
        def _(j):
            cols = pl.ds(pl.multiple_of(j * step, step), step)
            served = jnp.dot(
                active[pl.ds(0, count)], v[r, :, cols], preferred_element_type=F32
            )
            cot = c[span, cols].astype(F32)
            both = served * cot
            part = both[:, :128]
            for i in range(1, step // 128):
                part = part + both[:, i * 128 : (i + 1) * 128]
            sums[pl.ds(0, count)] += part
            o[span, cols] = (gate * served).astype(BF)
            c[span, cols] = (gate * cot).astype(BF)

        store(o.at[span], (hot_o, cold_o, copy_o)[r], r, 0)

        @pl.loop(0, count // tile)
        def _(i):
            rows = pl.ds(pl.multiple_of(i * tile, tile), tile)
            value = across(c[pl.ds(pl.multiple_of(first + i * tile, 128), tile)], v[r])
            slope[rows] = value * slope[rows]

        flat = jnp.sum(sums[pl.ds(0, count)], axis=1, keepdims=True)
        flat = jnp.transpose(jnp.broadcast_to(flat, (count, 128)))
        back_ref[:, first : first + count] = flat[:1]
        slanted = slope[pl.ds(0, count)]
        linear_grad = slanted.astype(BF)
        turned = jnp.transpose(slanted).astype(BF)
        active_turned = jnp.transpose(linear[pl.ds(0, count)]).astype(BF)

        @pl.loop(0, width // step)
        def _(j):
            cols = pl.ds(pl.multiple_of(j * step, step), step)
            q[span, cols] = across(linear_grad, u[r, cols]).astype(BF)
            w[r, :, cols] = jnp.dot(turned, x[span, cols], preferred_element_type=F32).astype(BF)
            w[3 + r, :, cols] = jnp.dot(
                active_turned, c[span, cols], preferred_element_type=F32
            ).astype(BF)

        store(q.at[span], (hot_g, cold_g, copy_g)[r], r, 1)
        store(w.at[r], grads_ref.at[r], r, 2)
        store(w.at[3 + r], grads_ref.at[3 + r], r, 3)
    for copy in stores:
        copy.wait()


def serve(hot, gathered, gates, up_weight, down_weight, copy_up, copy_down):
    width, hidden = up_weight.shape[1:]
    counts = [rows.shape[0] for rows in gathered[:3]]
    total = sum(counts)
    anywhere = pl.BlockSpec(memory_space=pl.ANY)
    vmem = pl.BlockSpec(memory_space=pltpu.VMEM)
    rows = [jax.ShapeDtypeStruct((count, width), BF) for count in counts]
    return pl.pallas_call(
        serve_kernel,
        out_shape=(
            *rows, *rows, jax.ShapeDtypeStruct((6, hidden, width), BF),
            jax.ShapeDtypeStruct((1, total), F32),
        ),
        in_specs=[pl.BlockSpec(memory_space=pltpu.SMEM)] + [anywhere] * 6 + [vmem] + [anywhere] * 4,
        out_specs=(anywhere,) * 7 + (vmem,),
        scratch_shapes=[
            pltpu.VMEM((total, width), BF),
            pltpu.VMEM((total, width), BF),
            pltpu.VMEM((3, width, hidden), BF),
            pltpu.VMEM((3, hidden, width), BF),
            pltpu.VMEM((total, width), BF),
            pltpu.VMEM((total, width), BF),
            pltpu.VMEM((6, hidden, width), BF),
            pltpu.VMEM((counts[0], hidden), F32),
            pltpu.VMEM((counts[0], hidden), F32),
            pltpu.VMEM((counts[0], hidden), BF),
            pltpu.VMEM((counts[0], 128), F32),
            pltpu.SemaphoreType.DMA((3, 4)),
            pltpu.SemaphoreType.DMA((3, 4)),
        ],
        compiler_params=pltpu.CompilerParams(vmem_limit_bytes=62 << 20),
        name="serve",
    )(hot, *gathered, gates, up_weight, down_weight, copy_up, copy_down)


class Place:
    def __init__(self):
        me = lax.axis_index("expert")
        self.me = me
        self.core = me % 2
        x = (me // 2) % SIDE
        y = me // (2 * SIDE)
        self.s = x * (1 - self.core) + y * self.core
        self.b = y * (1 - self.core) + x * self.core

    def at(self, db, ds):
        b = (self.b + db + SIDE) % SIDE
        s = (self.s + ds + SIDE) % SIDE
        y = b * (1 - self.core) + s * self.core
        x = s * (1 - self.core) + b * self.core
        return {"expert": (y * SIDE + x) * 2 + self.core}

    def partner(self):
        return {"expert": self.me + 1 - 2 * self.core}

    def replica(self, dz):
        return {"dp": (lax.axis_index("dp") + dz + REPLICAS) % REPLICAS}

    def before(self):
        return {"expert": (self.me + DEVICES - 1) % DEVICES}

    def beyond(self):
        return {"expert": (self.me + DEVICES - 1 + 2 * self.core) % DEVICES}


def greet(place, *more):
    barrier = pltpu.get_barrier_semaphore()
    others = [place.at(0, 1), place.at(0, -1), place.at(1, 0), place.at(-1, 0), place.partner()]
    others.extend(more)
    for other in others:
        pl.semaphore_signal(barrier, inc=1, device_id=other, device_id_type=pl.DeviceIdType.MESH)
    pl.semaphore_wait(barrier, len(others))


def remote(src, dst, send, recv, device):
    return pltpu.make_async_remote_copy(
        src_ref=src,
        dst_ref=dst,
        send_sem=send,
        recv_sem=recv,
        device_id=device,
        device_id_type=pl.DeviceIdType.MESH,
    )


def gather_kernel(
    tok_ref, cot_ref, pick_ref, hot_t, cold_t, copy_t, hot_c, cold_c, copy_c,
    held, rows, own_sem, send, recv, out_sem,
):
    place = Place()
    rows_of = tok_ref.shape[0]
    half = rows_of // 2
    width = tok_ref.shape[1]
    sources = (tok_ref, cot_ref)
    outs = ((hot_t, cold_t, copy_t), (hot_c, cold_c, copy_c))
    started = []
    greet(place)

    def start(copy):
        copy.start()
        started.append(copy)
        return copy

    def spot(a, db, ds, part=None):
        b = (place.b + db + SIDE) % SIDE
        s = (place.s + ds + SIDE) % SIDE
        first = pl.multiple_of(s * rows_of, rows_of)
        if part is None:
            return held.at[a, b, pl.ds(first, rows_of)]
        return held.at[a, b, pl.ds(pl.multiple_of(first + part * half, half), half)]

    def full_s(a, sign):
        return remote(
            sources[a], spot(a, 0, 0), send.at[0, 0, (1 - sign) // 2, a, 0],
            recv.at[0, 0, (1 - sign) // 2, a, 0], place.at(0, sign))

    def half_s(a, sign):
        part = (1 - sign) // 2
        return remote(
            spot(a, 0, -sign, part), spot(a, 0, -sign, part), send.at[1, 0, part, a, 0],
            recv.at[1, 0, part, a, 0], place.at(0, sign))

    def full_b(a, sign, ds):
        src = sources[a] if ds == 0 else spot(a, 0, ds)
        return remote(
            src, spot(a, 0, ds), send.at[0, 1, (1 - sign) // 2, a, ds % SIDE],
            recv.at[0, 1, (1 - sign) // 2, a, ds % SIDE], place.at(sign, 0))

    def half_b(a, sign, ds):
        part = (1 - sign) // 2
        return remote(
            spot(a, -sign, ds, part), spot(a, -sign, ds, part),
            send.at[1, 1, part, a, ds % SIDE], recv.at[1, 1, part, a, ds % SIDE],
            place.at(sign, 0))

    def pick(db):
        b = (place.b + db + SIDE) % SIDE
        slot = db % SIDE
        to = place.core * SIDE + b
        for a in range(2):

            @pl.loop(0, width // 512)
            def _(j):
                cols = pl.ds(pl.multiple_of(j * 512, 512), 512)
                rows[slot, a, :, cols] = jnp.dot(
                    pick_ref[b], held[a, b, :, cols], preferred_element_type=F32
                ).astype(BF)

            for r, (first, count) in enumerate(SPANS):
                copy = pltpu.make_async_copy(
                    rows.at[slot, a, pl.ds(first, count)], outs[a][r].at[to],
                    out_sem.at[0, slot, a, r])
                copy.start()
                kept.append(copy)
                start(
                    remote(
                        rows.at[slot, a, pl.ds(UNIT + first, count)], outs[a][r].at[to],
                        out_sem.at[1, slot, a, r], out_sem.at[2, slot, a, r],
                        place.partner()))

    kept = []
    for a in range(2):
        for sign in (1, -1):
            start(full_s(a, sign))
        for sign in (1, -1):
            start(full_b(a, sign, 0))
    for a in range(2):
        copy = pltpu.make_async_copy(sources[a], spot(a, 0, 0), own_sem.at[a])
        copy.start()
        kept.append(copy)
    for a in range(2):
        for sign in (1, -1):
            full_s(a, sign).wait_recv()
            start(half_s(a, sign))
            for way in (1, -1):
                start(full_b(a, way, -sign))
        for sign in (1, -1):
            full_b(a, sign, 0).wait_recv()
            start(half_b(a, sign, 0))
    for a in range(2):
        for sign in (1, -1):
            half_s(a, sign).wait_recv()
        for way in (1, -1):
            start(full_b(a, way, 2))
    for copy in kept:
        copy.wait()
    kept = []
    pick(0)
    for a in range(2):
        for ds in (-1, 1):
            for sign in (1, -1):
                full_b(a, sign, ds).wait_recv()
                start(half_b(a, sign, ds))
    for a in range(2):
        for sign in (1, -1):
            full_b(a, sign, 2).wait_recv()
            start(half_b(a, sign, 2))
    pick(1)
    pick(-1)
    for a in range(2):
        for ds in (0, -1, 1, 2):
            for sign in (1, -1):
                half_b(a, sign, ds).wait_recv()
    pick(2)
    for copy in kept:
        copy.wait()
    for slot in range(SIDE):
        for a in range(2):
            b = (place.b + slot) % SIDE
            to = (1 - place.core) * SIDE + b
            for r, (first, count) in enumerate(SPANS):
                remote(
                    rows.at[slot, a, pl.ds(UNIT + first, count)], outs[a][r].at[to],
                    out_sem.at[1, slot, a, r], out_sem.at[2, slot, a, r],
                    place.partner()).wait_recv()
    for copy in started:
        copy.wait_send()


def gather_rows(tokens, cotangent, picks):
    width = tokens.shape[1]
    rows_of = tokens.shape[0]
    shapes = [jax.ShapeDtypeStruct((2 * SIDE, count, width), BF) for _, count in SPANS]
    anywhere = pl.BlockSpec(memory_space=pl.ANY)
    return pl.pallas_call(
        gather_kernel,
        out_shape=tuple(shapes + shapes),
        in_specs=[anywhere, anywhere, pl.BlockSpec(memory_space=pltpu.VMEM)],
        out_specs=(anywhere,) * 6,
        scratch_shapes=[
            pltpu.VMEM((2, SIDE, SIDE * rows_of, width), BF),
            pltpu.VMEM((SIDE, 2, 2 * UNIT, width), BF),
            pltpu.SemaphoreType.DMA((2,)),
            pltpu.SemaphoreType.DMA((2, 2, 2, 2, SIDE)),
            pltpu.SemaphoreType.DMA((2, 2, 2, 2, SIDE)),
            pltpu.SemaphoreType.DMA((3, SIDE, 2, 3)),
        ],
        compiler_params=pltpu.CompilerParams(
            collective_id=0, has_side_effects=True, vmem_limit_bytes=60 << 20
        ),
        name="gather_rows",
    )(tokens, cotangent, picks)


def scatter_kernel(
    hot_o, cold_o, copy_o, hot_g, cold_g, copy_g, spread_ref, grads_ref,
    out_ref, grad_ref, up_ref, down_ref,
    rows, sums, first_in, second_in, third_in, fourth_in, parts, ring_in, copy_in,
    in_sem, send_r, recv_r, send_1, recv_1, send_2, recv_2, send_3, recv_3, send_4, recv_4,
    part_sem, send_z, recv_z, send_c, recv_c,
):
    place = Place()
    width = out_ref.shape[1]
    rows_of = out_ref.shape[0]
    half = rows_of // 2
    ins = ((hot_o, cold_o, copy_o), (hot_g, cold_g, copy_g))
    order = (2, 3, 1, 0)
    started = []
    greet(place, place.replica(1), place.replica(-1), place.beyond())

    def start(copy):
        copy.start()
        started.append(copy)

    def part_copy(d):
        z = (lax.axis_index("dp") + d) % REPLICAS
        piece = parts.shape[-1]
        return pltpu.make_async_copy(
            grads_ref.at[:, :, pl.ds(pl.multiple_of(z * piece, piece), piece)], parts.at[d],
            part_sem.at[d])

    def ring(sign, k, p):
        way = (1 - sign) // 2
        spot = p % 3 if k == 1 else 6 * k - 9 + p
        return remote(
            parts.at[(sign * (5 - k)) % REPLICAS, p], ring_in.at[way, spot],
            send_z.at[way, spot], recv_z.at[way, spot], place.replica(sign))

    def later(sign):
        return (0, 1, 2) if sign == 1 else (3, 4, 5)

    def ring_start():
        for d in (4, 3, 5, 2, 6, 1, 7, 0):
            part_copy(d).start()
        part_copy(4).wait()
        for i in range(3):
            for sign in (1, -1):
                start(ring(sign, 1, later(sign)[i]))
        part_copy(3).wait()
        part_copy(5).wait()
        for i in range(3):
            for sign in (1, -1):
                start(ring(sign, 2, later(-sign)[i]))
        for d in (2, 6, 1, 7, 0):
            part_copy(d).wait()

    def ring_step(k, second):
        for i in range(3):
            for sign in (1, -1):
                p = later(sign if second else -sign)[i]
                ring(sign, k, p).wait_recv()
                spot = p % 3 if k == 1 else 6 * k - 9 + p
                add(parts.at[(sign * (4 - k)) % REPLICAS, p], ring_in.at[(1 - sign) // 2, spot])
                start(ring(sign, k + 1, p))

    def hand_over(i):
        return remote(
            parts.at[0, 3 * i + 2], copy_in.at[i], send_c.at[i], recv_c.at[i], place.before())

    def ring_end(p):
        for sign in (1, -1):
            ring(sign, 4, p).wait_recv()
        spot = 15 + p
        if p % 3 == 2:
            add(parts.at[0, p], ring_in.at[0, spot], ring_in.at[1, spot])
            start(hand_over(p // 3))
            return
        total = parts[0, p].astype(F32)
        for way in range(2):
            total = total + ring_in[way, spot].astype(F32)
        if p % 3 == 0:
            hand_over(p // 3).wait_recv()
            total = total + copy_in[p // 3].astype(F32)
        if p < 3:
            up_ref[p] = jnp.transpose(total).astype(BF)
        else:
            down_ref[p - 3] = total.astype(BF)

    def unit_copies(slot, a, r):
        first, count = SPANS[r]
        b = (place.b + slot) % SIDE
        return pltpu.make_async_copy(
            ins[a][r].at[place.core * SIDE + b], rows.at[slot, a, pl.ds(first, count)],
            in_sem.at[slot, a, r])

    def unit_sends(slot, a, r):
        first, count = SPANS[r]
        b = (place.s + slot) % SIDE
        return remote(
            ins[a][r].at[(1 - place.core) * SIDE + b],
            rows.at[slot, a, pl.ds(UNIT + first, count)],
            send_r.at[slot, a, r], recv_r.at[slot, a, r], place.partner())

    def chunk(slot, a, ds, part=None):
        s = (place.s + ds + SIDE) % SIDE
        first = pl.multiple_of(s * rows_of, rows_of)
        if part is None:
            return sums.at[slot, a, pl.ds(first, rows_of)]
        return sums.at[slot, a, pl.ds(pl.multiple_of(first + part * half, half), half)]

    def far(slot, a, sign):
        part = (1 - sign) // 2
        return remote(
            chunk(slot, a, 2, part), first_in.at[slot, a, part],
            send_1.at[slot, a, part], recv_1.at[slot, a, part], place.at(0, sign))

    def near(slot, a, sign, part):
        way = (1 - sign) // 2
        return remote(
            chunk(slot, a, sign, part), second_in.at[slot, a, way, pl.ds(part * half, half)],
            send_2.at[slot, a, way, part], recv_2.at[slot, a, way, part],
            place.at(0, sign))

    def far_b(a, sign):
        part = (1 - sign) // 2
        return remote(
            chunk(2, a, 0, part), third_in.at[a, part],
            send_3.at[a, part], recv_3.at[a, part], place.at(sign, 0))

    def near_b(a, sign, part):
        way = (1 - sign) // 2
        return remote(
            chunk(sign % SIDE, a, 0, part), fourth_in.at[a, way, pl.ds(part * half, half)],
            send_4.at[a, way, part], recv_4.at[a, way, part], place.at(sign, 0))

    def add(into, *others):
        @pl.loop(0, into.shape[0] // 32)
        def _(i):
            span = pl.ds(pl.multiple_of(i * 32, 32), 32)
            total = into[span].astype(F32)
            for other in others:
                total = total + other[span].astype(F32)
            into[span] = total.astype(BF)

    for slot in order:
        for a in range(2):
            for r in range(3):
                start(unit_sends(slot, a, r))
                unit_copies(slot, a, r).start()

    def expand(slot):
        b = (place.b + slot) % SIDE
        for a in range(2):
            for r in range(3):
                unit_copies(slot, a, r).wait()
                unit_sends(slot, a, r).wait_recv()

            @pl.loop(0, width // 512)
            def _(j):
                cols = pl.ds(pl.multiple_of(j * 512, 512), 512)
                sums[slot, a, :, cols] = jnp.dot(
                    spread_ref[b], rows[slot, a, :, cols], preferred_element_type=F32
                ).astype(BF)

            for sign in (1, -1):
                start(far(slot, a, sign))
            for sign in (1, -1):
                start(near(slot, a, sign, (1 + sign) // 2))

    def pass_on(slot):
        for a in range(2):
            for sign in (1, -1):
                part = (1 - sign) // 2
                far(slot, a, sign).wait_recv()
                add(chunk(slot, a, sign, part), first_in.at[slot, a, part])
                start(near(slot, a, sign, part))

    def finish(slot):
        for a in range(2):
            for sign in (1, -1):
                for part in range(2):
                    near(slot, a, sign, part).wait_recv()
            add(chunk(slot, a, 0), second_in.at[slot, a, 0], second_in.at[slot, a, 1])

    ring_start()
    expand(2)
    expand(3)
    pass_on(2)
    ring_step(1, True)
    expand(1)
    ring_step(2, False)
    pass_on(3)
    finish(2)
    for a in range(2):
        for sign in (1, -1):
            start(far_b(a, sign))
    expand(0)
    ring_step(2, True)
    pass_on(1)
    finish(3)
    for a in range(2):
        start(near_b(a, -1, 0))
    ring_step(3, False)
    pass_on(0)
    finish(1)
    for a in range(2):
        start(near_b(a, 1, 1))
    ring_step(3, True)
    for a in range(2):
        for sign in (1, -1):
            part = (1 - sign) // 2
            far_b(a, sign).wait_recv()
            add(chunk(sign % SIDE, a, 0, part), third_in.at[a, part])
            start(near_b(a, sign, part))
    finish(0)
    for p in (5, 2):
        ring_end(p)
    for a, result in ((0, out_ref), (1, grad_ref)):
        for sign in (1, -1):
            for part in range(2):
                near_b(a, sign, part).wait_recv()
        own = chunk(0, a, 0)
        result[...] = (
            own[...].astype(F32) + fourth_in[a, 0].astype(F32) + fourth_in[a, 1].astype(F32)
        ).astype(BF)
    for p in (4, 1, 3, 0):
        ring_end(p)
    for copy in started:
        copy.wait_send()


def scatter_rows(out_rows, grad_rows, spread, grads, rows_of):
    width = out_rows[0].shape[-1]
    hidden = grads.shape[1]
    piece = width // REPLICAS
    half = rows_of // 2
    anywhere = pl.BlockSpec(memory_space=pl.ANY)
    vmem = pl.BlockSpec(memory_space=pltpu.VMEM)
    shape = jax.ShapeDtypeStruct((rows_of, width), BF)
    dma = pltpu.SemaphoreType.DMA
    return pl.pallas_call(
        scatter_kernel,
        out_shape=(
            shape, shape, jax.ShapeDtypeStruct((2, piece, hidden), BF),
            jax.ShapeDtypeStruct((2, hidden, piece), BF),
        ),
        in_specs=[anywhere] * 6 + [vmem, anywhere],
        out_specs=(vmem,) * 4,
        scratch_shapes=[
            pltpu.VMEM((SIDE, 2, 2 * UNIT, width), BF),
            pltpu.VMEM((SIDE, 2, SIDE * rows_of, width), BF),
            pltpu.VMEM((SIDE, 2, 2, half, width), BF),
            pltpu.VMEM((SIDE, 2, 2, rows_of, width), BF),
            pltpu.VMEM((2, 2, half, width), BF),
            pltpu.VMEM((2, 2, rows_of, width), BF),
            pltpu.VMEM((REPLICAS, 6, hidden, piece), BF),
            pltpu.VMEM((2, 21, hidden, piece), BF),
            pltpu.VMEM((2, hidden, piece), BF),
            dma((SIDE, 2, 3)),
            dma((SIDE, 2, 3)),
            dma((SIDE, 2, 3)),
            dma((SIDE, 2, 2)),
            dma((SIDE, 2, 2)),
            dma((SIDE, 2, 2, 2)),
            dma((SIDE, 2, 2, 2)),
            dma((2, 2)),
            dma((2, 2)),
            dma((2, 2, 2)),
            dma((2, 2, 2)),
            dma((REPLICAS,)),
            dma((2, 21)),
            dma((2, 21)),
            dma((2,)),
            dma((2,)),
        ],
        compiler_params=pltpu.CompilerParams(
            collective_id=1, has_side_effects=True, vmem_limit_bytes=67043328
        ),
        name="scatter_rows",
    )(*out_rows, *grad_rows, spread, grads)


def regions(values, fill):
    lead = values.shape[:-2]
    hot = values[..., :HOT].reshape(*lead, HOT_U)
    cold = values[..., HOT : HOT + COLD].reshape(*lead, COLD_U)
    copied = values[..., HOT + COLD : HOT + COLD + COPY].reshape(*lead, SIDE * COPY)
    pad = [(0, 0)] * len(lead) + [(0, COPY_U - SIDE * COPY)]
    return hot, cold, jnp.pad(copied, pad, constant_values=fill)


def local(
    tokens,
    cotangent,
    gate_weights,
    expert_ids,
    copy_pick,
    copy_expert,
    up_weight,
    down_weight,
    copy_up,
    copy_down,
):
    devices = lax.axis_size("expert")
    me = lax.axis_index("expert")
    core = me % 2
    rows_of, width = tokens.shape
    table, dest, slot = route(expert_ids.T, copy_pick.T, gate_weights.T, copy_expert)
    sent = jnp.broadcast_to(
        table.reshape(devices // 2, 1, 2, 128), (devices // 2, 2, 2, 128)
    ).reshape(devices, 2, 128)
    tables = lax.all_to_all(sent, "expert", split_axis=0, concat_axis=0, tiled=True)
    grid = tables.reshape(SIDE, SIDE, 2, 2, 128)
    by_unit = jnp.stack([grid[:, :, 0], jnp.swapaxes(grid[:, :, 1], 0, 1)])
    mine = jnp.where(core == 0, by_unit[:, :, :, 0], by_unit[:, :, :, 1])
    gates = regions(mine[..., 64 : 64 + SLOTS], 0.0)
    named = jnp.where(core == 0, by_unit[0], by_unit[1])[..., :SLOTS].astype(jnp.int32)
    named = jnp.where(core == 0, named, named[:, :, ::-1])
    place = jnp.arange(SIDE, dtype=jnp.int32)[None, :, None, None] * rows_of
    named = jnp.where(named > 0, place + named - 1, -1)
    named = jnp.concatenate(regions(jnp.moveaxis(named, 2, 1), -1), axis=-1)
    named = named.reshape(SIDE, 2 * UNIT)
    sites = jnp.arange(SIDE * rows_of, dtype=jnp.int32)
    picks = (named[:, :, None] == sites[None, None, :]).astype(BF)
    spread = (named[:, None, :] == sites[None, :, None]).astype(BF)

    gathered = gather_rows(tokens, cotangent, picks)
    hot_slot = copy_expert[(me + 1) % devices] % 2
    gates = jnp.concatenate([gate.reshape(1, -1) for gate in gates], axis=1)
    *rows, grads, back = serve(
        hot_slot.reshape(1),
        [part.reshape(-1, width) for part in gathered],
        gates, up_weight, down_weight, copy_up, copy_down,
    )
    rows = [part.reshape(2 * SIDE, -1, width) for part in rows]
    layer_output, token_grad, up_parts, down_parts = scatter_rows(
        rows[:3], rows[3:], spread, grads, rows_of
    )

    hot_back, cold_back, copy_back = jnp.split(
        back[0], [2 * SIDE * HOT_U, 2 * SIDE * (HOT_U + COLD_U)]
    )
    by_slot = jnp.concatenate(
        [
            hot_back.reshape(2, SIDE, SIDE, HOT),
            cold_back.reshape(2, SIDE, SIDE, COLD),
            copy_back.reshape(2, SIDE, COPY_U)[:, :, : SIDE * COPY].reshape(2, SIDE, SIDE, COPY),
        ],
        axis=-1,
    )
    by_source = jnp.stack([by_slot[0], jnp.swapaxes(by_slot[1], 0, 1)], axis=2)
    by_source = jnp.pad(
        by_source.reshape(devices, HOT + COLD + COPY), ((0, 0), (0, 128 - HOT - COLD - COPY))
    )
    returned = lax.all_to_all(by_source, "expert", split_axis=0, concat_axis=0, tiled=True)
    gate_grad = gate_back(dest, slot, returned).T

    up_grad = jnp.where(hot_slot == 0, up_parts, up_parts[::-1])
    down_grad = jnp.where(hot_slot == 0, down_parts, down_parts[::-1])
    return layer_output, token_grad, gate_grad, up_grad, down_grad


def solution(mesh):
    rows = P(("expert", "dp"), None)
    held = P("expert", None, None)
    return jax.shard_map(
        local,
        mesh=mesh,
        in_specs=(rows,) * 5 + (P(),) + (held,) * 4,
        out_specs=(rows, rows, rows, P("expert", "dp", None), P("expert", None, "dp")),
        check_vma=False,
    )
```

profile of v0, /device:TPU:5, one launch (start us, length us, event | category | flops | bytes accessed | tf_op | source)
XLA Modules:
  0.0 285.0 jit_solution(3683710178924010133)
XLA Ops:
  0.6 1.3 copy.46.listed_ref
  2.0 3.8 %route.1 = (f32[32,128]{1,0:T(8,128)}, s32[8,128]{1,0:T(8,128)}, s32[8,128]{1,0:T(8,128)}) custom-call(s32[8,128]{1,0:T(8,128)} %bitcast.72, s32[8,128]{1,0:T(8,128)} %bitcast.73, f32[8,128]{1,0:T(8,128)} %bitcast.74, s32[32,1]{1,0:T(8,128)} %copy.46.listed_ref), custom_call_target="tpu_custom_call" | custom-call | tf_op jit(solution)/shard_map/route/pallas_call | solution.py:65
  5.8 1.3 broadcast_in_dim.7
  7.1 7.9 %all-to-all-start = ((f32[32,2,128]{2,1,0:T(2,128)}), f32[32,2,128]{2,1,0:T(2,128)S(1)}, u32[]{:S(2)}, u32[]{:S(2)}) async-start(f32[32,2,128]{2,1,0:T(2,128)} %bitcast.7), calls=%async_computation | async-start | bytes 65536 | tf_op jit(solution)/shard_map/all_to_all | solution.py:756
  15.1 1.2 dynamic_slice.3
  18.3 2.0 all-to-all-done
  20.4 0.1 select_bitcast_fusion
  20.4 0.1 slice.68
  20.5 0.1 slice.69
  20.6 0.1 slice.74
  20.7 0.1 slice.72
  20.8 0.1 slice.73
  20.8 0.1 reshape.112
  20.9 0.1 reshape.113
  21.0 0.1 reshape.111
  21.1 0.1 fusion.6
  21.2 0.1 eq.42
  21.3 1.5 fusion.1.pick_ref
  22.8 0.1 reshape.120
  22.9 0.1 reshape.121
  23.0 0.1 reshape_reshape.6
  23.1 0.1 reshape_reshape.7
  23.2 96.9 %gather_rows.1 = (bf16[8,96,2048]{2,1,0:T(8,128)(2,1)}, bf16[8,48,2048]{2,1,0:T(8,128)(2,1)}, bf16[8,32,2048]{2,1,0:T(8,128)(2,1)}, bf16[8,96,2048]{2,1,0:T(8,12...) custom-call(bf16[128,2048]{1,0:T(8,128)(2,1)} %tok_ref.1, bf16[128,2048]{1,0:T(8,128)(2,1)} %cot_ref.1, ...), custom_call_target="tpu_custom_call" | custom-call | tf_op jit(solution)/shard_map/gather_rows/pallas_call | solution.py:429
  120.1 0.6 pad_maximum_fusion.3.gates_ref
  120.7 30.1 %serve.1 = (bf16[768,2048]{1,0:T(8,128)(2,1)}, bf16[384,2048]{1,0:T(8,128)(2,1)}, bf16[256,2048]{1,0:T(8,128)(2,1)}, bf16[768,2048]{1,0:T(8,128)(2,1)}, bf16[384...) custom-call(s32[1]{0:T(128)} %bitcast.1.which_ref, ...), custom_call_target="tpu_custom_call" | custom-call | tf_op jit(solution)/shard_map/serve/pallas_call | solution.py:212
  150.8 0.7 slice_reduce_fusion.2
  151.5 0.7 slice_reduce_fusion
  152.2 0.7 slice_reduce_fusion.1
  152.9 1.6 fusion.spread_ref
  154.5 0.1 reshape.130
  154.5 0.1 reshape.131
  154.6 0.1 reshape.128
  154.7 0.1 reshape.129
  154.8 0.1 pad_maximum_fusion.1
  155.0 0.6 pad.14
  155.6 6.3 %all-to-all-start.1 = ((f32[32,1,128]{2,1,0:T(1,128)}), f32[32,1,128]{2,1,0:T(1,128)}, u32[]{:S(2)}, u32[]{:S(2)}) async-start(f32[32,1,128]{2,1,0:T(1,128)} %bitcast.34), calls=%async_computation.1 | async-start | bytes 32768 | tf_op jit(solution)/shard_map/all_to_all | solution.py:799
  161.9 114.4 %scatter_rows.1 = (bf16[128,2048]{1,0:T(8,128)(2,1)}, bf16[128,2048]{1,0:T(8,128)(2,1)}, bf16[2,256,384]{2,1,0:T(8,128)(2,1)}, bf16[2,384,256]{2,1,0:T(8,128)(2,1)}) custom-call(bf16[8,96,2048]{2,1,0:T(8,128)(2,1)} %bitcast.52, bf16[8,48,2048]{2,1,0:T(8,128)(2,1)} %bitcast.56, bf16[8,32,2048]{2,1,0:T(8,128)(2,1)} %bitcast.58, bf16[8,96,2048]{2,1,0:T(8,128)(2,1)} %bitcast.53, ...), custom_call_target="tpu_custom_call" | custom-call | tf_op jit(solution)/shard_map/scatter_rows/pallas_call | solution.py:685
  276.3 0.0 copy-start
  276.4 2.1 reverse_select_fusion
  278.4 2.0 reverse_select_fusion.1
  280.4 0.0 all-to-all-done.1
  280.4 2.0 gate_back.1
  282.3 1.9 copy.66
  284.2 0.0 copy-done
  284.2 0.8 copy.67
  (17 shorter events, 0.1 us)
Async XLA Ops:
  7.1 13.2 %all-to-all-start = ((f32[32,2,128]{2,1,0:T(2,128)}), f32[32,2,128]{2,1,0:T(2,128)S(1)}, u32[]{:S(2)}, u32[]{:S(2)}) async-start(f32[32,2,128]{2,1,0:T(2,128)} %bitcast.7), calls=%async_computation | async-start | bytes 65536 | tf_op jit(solution)/shard_map/all_to_all | solution.py:756
  155.6 124.8 %all-to-all-start.1 = ((f32[32,1,128]{2,1,0:T(1,128)}), f32[32,1,128]{2,1,0:T(1,128)}, u32[]{:S(2)}, u32[]{:S(2)}) async-start(f32[32,1,128]{2,1,0:T(1,128)} %bitcast.34), calls=%async_computation.1 | async-start | bytes 32768 | tf_op jit(solution)/shard_map/all_to_all | solution.py:799
  276.3 7.9 %copy-start = (bf16[128,2048]{1,0:T(8,128)(2,1)S(1)}, bf16[128,2048]{1,0:T(8,128)(2,1)}, u32[]{:S(2)}) copy-start(bf16[128,2048]{1,0:T(8,128)(2,1)} %get-tuple-element.59) | copy-start | bytes 1572868
where the time goes:
time: 287 us; the launch traced here: 285 us
  Pallas kernels  247 us (86%)
  starting transfers between devices  14.2 us (5%)
  local copies, waits for them, and re-layouts  10.9 us (4%)
  other arithmetic  7.97 us (3%)
    pallas_call x1, Pallas kernels, scatter_rows(): pl.pallas_call(scatter_kernel, out_shape=(shape, shape, jax.ShapeDtypeStr...  114 us
    pallas_call x1, Pallas kernels, gather_rows(): pl.pallas_call(gather_kernel, out_shape=tuple(shapes + shapes), in_specs=...  96.9 us
    pallas_call x1, Pallas kernels, serve(): pl.pallas_call(serve_kernel, out_shape=(*rows, *rows, jax.ShapeDtypeStruc...  30.1 us
    all_to_all x1, starting transfers between devices, local(): lax.all_to_all(sent, 'expert', split_axis=0, concat_axis=0, tiled=True)  7.88 us
    all_to_all x1, starting transfers between devices, local(): lax.all_to_all(by_source, 'expert', split_axis=0, concat_axis=0, tiled=True)  6.28 us
  transfers between devices with their start and end apart: 2, of which 1 were waited for; matrix products, arithmetic and copies ran while one was open for 2% of the time, Pallas kernels for 40%

commit v1 on v0

--- a/solution.py
+++ b/solution.py
@@ -27,8 +27,10 @@
 def route_kernel(ids_ref, picks_ref, gates_ref, listed_ref, table_ref, dest_ref, slot_ref):
     chosen, rows = ids_ref.shape
     ids, picks, gates = ids_ref[...], picks_ref[...], gates_ref[...]
-    listed = listed_ref[...]
-    devices = listed.shape[0]
+    devices = listed_ref.shape[0]
+    cold = jnp.ones((chosen, rows), jnp.int32)
+    for i in range(devices):
+        cold = jnp.where(ids == listed_ref[i], 0, cold)
     before = (iota((rows, rows), 0) < iota((rows, rows), 1)).astype(BF)
     lines = iota((128, rows), 0)
     token = iota((128, rows), 1).astype(F32) + 1.0
@@ -36,9 +38,8 @@
     table = jnp.zeros((devices, 128), F32)
     for k in range(chosen):
         e, p, g = ids[k : k + 1], picks[k : k + 1], gates[k : k + 1]
-        hot = jnp.max((e == listed).astype(jnp.int32), axis=0, keepdims=True)
         dest = (e // 2 + p) % devices
-        region = jnp.where(p == 1, 2, 1 - hot)
+        region = jnp.where(p == 1, 2, cold[k : k + 1])
         hit = (region * devices + dest == lines).astype(F32)
         ahead = jnp.dot(hit.astype(BF), before, preferred_element_type=F32) + offset
         rank = jnp.sum(hit * ahead, axis=0, keepdims=True).astype(jnp.int32)
@@ -69,10 +70,19 @@
             jax.ShapeDtypeStruct((chosen, rows), jnp.int32),
             jax.ShapeDtypeStruct((chosen, rows), jnp.int32),
         ),
-        in_specs=[vmem] * 4,
+        in_specs=[vmem] * 3 + [pl.BlockSpec(memory_space=pltpu.SMEM)],
         out_specs=(vmem,) * 3,
         name="route",
-    )(ids, picks, gates, listed.reshape(-1, 1))
+    )(ids, picks, gates, listed)
+
+
+def seats(s, rows, lead):
+    row, lane = iota((rows, 128), 0), iota((rows, 128), 1) - lead
+    hot = (row - HOT * s == lane) & (lane >= 0) & (lane < HOT)
+    cold = (row - HOT_U - COLD * s == lane - HOT) & (lane >= HOT) & (lane < HOT + COLD)
+    copied = (row - HOT_U - COLD_U - COPY * s == lane - HOT - COLD) & (lane >= HOT + COLD)
+    copied = copied & (lane < HOT + COLD + COPY)
+    return (hot | cold | copied).astype(F32)
 
 
 def gate_kernel(dest_ref, slot_ref, back_ref, out_ref):
@@ -100,13 +110,14 @@
 def serve_kernel(
     which_ref, hot_t, cold_t, copy_t, hot_c, cold_c, copy_c, gates_ref, up_ref, down_ref,
     copy_up_ref, copy_down_ref, hot_o, cold_o, copy_o, hot_g, cold_g, copy_g, grads_ref, back_ref,
-    x, c, u, v, o, q, w, linear, slope, active, sums, in_sem, out_sem,
+    x, c, u, v, o, q, w, linear, slope, active, sums, gate_cols, by_unit, in_sem, out_sem,
 ):
     firsts = (0, hot_t.shape[0], hot_t.shape[0] + cold_t.shape[0])
     counts = (hot_t.shape[0], cold_t.shape[0], copy_t.shape[0])
     width = x.shape[1]
     step = 512
-    hot = which_ref[0]
+    me = lax.axis_index("expert")
+    hot = which_ref[(me + 1) % DEVICES] % 2
     ups = (up_ref.at[hot], up_ref.at[1 - hot], copy_up_ref.at[0])
     downs = (down_ref.at[hot], down_ref.at[1 - hot], copy_down_ref.at[0])
 
@@ -130,12 +141,16 @@
     for r in (2, 1, 0):
         for copy in loads(r):
             copy.start()
+    for i in range(2 * SIDE):
+        columns = jnp.transpose(jnp.broadcast_to(gates_ref[i, :1], (128, gates_ref.shape[2])))
+        for r, (low, rows) in enumerate(SPANS):
+            gate_cols[pl.ds(firsts[r] + i * rows, rows)] = columns[low : low + rows]
+    by_unit[...] = jnp.zeros_like(by_unit)
     for r in (2, 1, 0):
         first, count = firsts[r], counts[r]
         span = pl.ds(first, count)
         ready = loads(r)
-        gate = jnp.transpose(jnp.broadcast_to(gates_ref[:, first : first + count], (128, count)))
-        gate = gate[:, :1]
+        gate = gate_cols[span][:, :1]
         ready[0].wait()
         ready[1].wait()
         tile = min(count, 384)
@@ -178,9 +193,12 @@
             value = across(c[pl.ds(pl.multiple_of(first + i * tile, 128), tile)], v[r])
             slope[rows] = value * slope[rows]
 
-        flat = jnp.sum(sums[pl.ds(0, count)], axis=1, keepdims=True)
-        flat = jnp.transpose(jnp.broadcast_to(flat, (count, 128)))
-        back_ref[:, first : first + count] = flat[:1]
+        low, rows = SPANS[r]
+        totals = jnp.zeros((rows, 128), F32)
+        for i in range(2 * SIDE):
+            one = jnp.sum(sums[pl.ds(i * rows, rows)], axis=1, keepdims=True)
+            totals = jnp.where(iota((rows, 128), 1) == i, one, totals)
+        by_unit[pl.ds(low, rows)] = totals
         slanted = slope[pl.ds(0, count)]
         linear_grad = slanted.astype(BF)
         turned = jnp.transpose(slanted).astype(BF)
@@ -198,11 +216,21 @@
         store(q.at[span], (hot_g, cold_g, copy_g)[r], r, 1)
         store(w.at[r], grads_ref.at[r], r, 2)
         store(w.at[3 + r], grads_ref.at[3 + r], r, 3)
+    turned = jnp.transpose(by_unit[...])
+    for s in range(SIDE):
+        lines = jnp.dot(
+            turned, seats(s, by_unit.shape[0], 0), precision=EXACT, preferred_element_type=F32
+        )
+        for b in range(SIDE):
+            for core in range(2):
+                source = ((b * SIDE + s) if core == 0 else (s * SIDE + b)) * 2 + core
+                i = core * SIDE + b
+                back_ref[source : source + 1] = lines[i : i + 1]
     for copy in stores:
         copy.wait()
 
 
-def serve(hot, gathered, gates, up_weight, down_weight, copy_up, copy_down):
+def serve(listed, gathered, gates, up_weight, down_weight, copy_up, copy_down):
     width, hidden = up_weight.shape[1:]
     counts = [rows.shape[0] for rows in gathered[:3]]
     total = sum(counts)
@@ -213,7 +241,7 @@
         serve_kernel,
         out_shape=(
             *rows, *rows, jax.ShapeDtypeStruct((6, hidden, width), BF),
-            jax.ShapeDtypeStruct((1, total), F32),
+            jax.ShapeDtypeStruct((DEVICES, 128), F32),
         ),
         in_specs=[pl.BlockSpec(memory_space=pltpu.SMEM)] + [anywhere] * 6 + [vmem] + [anywhere] * 4,
         out_specs=(anywhere,) * 7 + (vmem,),
@@ -229,12 +257,14 @@
             pltpu.VMEM((counts[0], hidden), F32),
             pltpu.VMEM((counts[0], hidden), BF),
             pltpu.VMEM((counts[0], 128), F32),
+            pltpu.VMEM((total, 128), F32),
+            pltpu.VMEM((256, 128), F32),
             pltpu.SemaphoreType.DMA((3, 4)),
             pltpu.SemaphoreType.DMA((3, 4)),
         ],
         compiler_params=pltpu.CompilerParams(vmem_limit_bytes=62 << 20),
         name="serve",
-    )(hot, *gathered, gates, up_weight, down_weight, copy_up, copy_down)
+    )(listed, *gathered, gates, up_weight, down_weight, copy_up, copy_down)
 
 
 class Place:
@@ -288,14 +318,13 @@
 
 
 def gather_kernel(
-    tok_ref, cot_ref, pick_ref, hot_t, cold_t, copy_t, hot_c, cold_c, copy_c,
-    held, rows, own_sem, send, recv, out_sem,
+    tok_ref, cot_ref, table_ref, hot_t, cold_t, copy_t, hot_c, cold_c, copy_c, gates_ref, spread_ref,
+    held, tables, rows, picks, spread, gates, own_sem, send, recv, out_sem, gate_sem, spread_sem,
 ):
     place = Place()
     rows_of = tok_ref.shape[0]
-    half = rows_of // 2
     width = tok_ref.shape[1]
-    sources = (tok_ref, cot_ref)
+    sources = (tok_ref, cot_ref, table_ref)
     outs = ((hot_t, cold_t, copy_t), (hot_c, cold_c, copy_c))
     started = []
     greet(place)
@@ -308,10 +337,13 @@
     def spot(a, db, ds, part=None):
         b = (place.b + db + SIDE) % SIDE
         s = (place.s + ds + SIDE) % SIDE
-        first = pl.multiple_of(s * rows_of, rows_of)
+        count = sources[a].shape[0]
+        half = count // 2
+        first = pl.multiple_of(s * count, count)
+        within = tables.at[b] if a == 2 else held.at[a, b]
         if part is None:
-            return held.at[a, b, pl.ds(first, rows_of)]
-        return held.at[a, b, pl.ds(pl.multiple_of(first + part * half, half), half)]
+            return within.at[pl.ds(first, count)]
+        return within.at[pl.ds(pl.multiple_of(first + part * half, half), half)]
 
     def full_s(a, sign):
         return remote(
@@ -337,42 +369,78 @@
             send.at[1, 1, part, a, ds % SIDE], recv.at[1, 1, part, a, ds % SIDE],
             place.at(sign, 0))
 
-    def pick(db):
+    def plan(db):
         b = (place.b + db + SIDE) % SIDE
         slot = db % SIDE
-        to = place.core * SIDE + b
-        for a in range(2):
+        for h in range(2):
+            target = place.me + h * (1 - 2 * place.core)
+            scale = jnp.zeros((8, UNIT), F32)
+            for s in range(SIDE):
+                line = tables[b, pl.ds(s * DEVICES + target, 1), :]
+                wide = jnp.broadcast_to(line, (128, 128))
+                site = iota((128, 128), 1).astype(F32) + 1.0
+                one = (jnp.transpose(wide) == site).astype(BF)
+                turned = (wide == iota((128, 128), 0).astype(F32) + 1.0).astype(BF)
+                seat = seats(s, UNIT, 0).astype(BF)
+                span = pl.ds(s * rows_of, rows_of)
+                picks[slot, h, :, span] = jnp.dot(seat, one, preferred_element_type=F32).astype(BF)
+                spread[slot, h, span, :] = across(turned, seat).astype(BF)
+                scale = scale + across(wide[:8], seats(s, UNIT, 64), EXACT)
+            gates[slot, h, :, pl.ds(0, UNIT)] = scale
+        unit = place.core * SIDE + b
+        keep(pltpu.make_async_copy(gates.at[slot, 0], gates_ref.at[unit], gate_sem.at[0, slot]))
+        start(gates_out(slot))
+        keep(pltpu.make_async_copy(spread.at[slot], spread_ref.at[b], spread_sem.at[slot]))
+
+    def gates_out(slot):
+        b = (place.b + slot) % SIDE
+        return remote(
+            gates.at[slot, 1], gates_ref.at[place.core * SIDE + b], gate_sem.at[1, slot],
+            gate_sem.at[2, slot], place.partner())
+
+    def rows_out(slot, a, r):
+        b = (place.b + slot) % SIDE
+        first, count = SPANS[r]
+        return remote(
+            rows.at[slot, a, 1, pl.ds(first, count)], outs[a][r].at[place.core * SIDE + b],
+            out_sem.at[1, slot, a, r], out_sem.at[2, slot, a, r], place.partner())
+
+    def pick(db, a):
+        b = (place.b + db + SIDE) % SIDE
+        slot = db % SIDE
+        for h in (1, 0):
 
             @pl.loop(0, width // 512)
             def _(j):
                 cols = pl.ds(pl.multiple_of(j * 512, 512), 512)
-                rows[slot, a, :, cols] = jnp.dot(
-                    pick_ref[b], held[a, b, :, cols], preferred_element_type=F32
+                rows[slot, a, h, :, cols] = jnp.dot(
+                    picks[slot, h], held[a, b, :, cols], preferred_element_type=F32
                 ).astype(BF)
 
             for r, (first, count) in enumerate(SPANS):
-                copy = pltpu.make_async_copy(
-                    rows.at[slot, a, pl.ds(first, count)], outs[a][r].at[to],
-                    out_sem.at[0, slot, a, r])
-                copy.start()
-                kept.append(copy)
-                start(
-                    remote(
-                        rows.at[slot, a, pl.ds(UNIT + first, count)], outs[a][r].at[to],
-                        out_sem.at[1, slot, a, r], out_sem.at[2, slot, a, r],
-                        place.partner()))
+                if h == 1:
+                    start(rows_out(slot, a, r))
+                else:
+                    keep(
+                        pltpu.make_async_copy(
+                            rows.at[slot, a, 0, pl.ds(first, count)],
+                            outs[a][r].at[place.core * SIDE + b], out_sem.at[0, slot, a, r]))
 
     kept = []
-    for a in range(2):
-        for sign in (1, -1):
-            start(full_s(a, sign))
-        for sign in (1, -1):
-            start(full_b(a, sign, 0))
-    for a in range(2):
-        copy = pltpu.make_async_copy(sources[a], spot(a, 0, 0), own_sem.at[a])
+
+    def keep(copy):
         copy.start()
         kept.append(copy)
-    for a in range(2):
+
+    arrays = (2, 0, 1)
+    for a in arrays:
+        for sign in (1, -1):
+            start(full_s(a, sign))
+        for sign in (1, -1):
+            start(full_b(a, sign, 0))
+    for a in arrays:
+        keep(pltpu.make_async_copy(sources[a], spot(a, 0, 0), own_sem.at[a]))
+    for a in arrays:
         for sign in (1, -1):
             full_s(a, sign).wait_recv()
             start(half_s(a, sign))
@@ -381,77 +449,87 @@
         for sign in (1, -1):
             full_b(a, sign, 0).wait_recv()
             start(half_b(a, sign, 0))
-    for a in range(2):
+    for a in arrays:
         for sign in (1, -1):
             half_s(a, sign).wait_recv()
         for way in (1, -1):
             start(full_b(a, way, 2))
     for copy in kept:
         copy.wait()
-    kept = []
-    pick(0)
+    kept.clear()
+    plan(0)
     for a in range(2):
-        for ds in (-1, 1):
+        pick(0, a)
+    for ds in (-1, 1, 2):
+        for a in arrays:
             for sign in (1, -1):
                 full_b(a, sign, ds).wait_recv()
                 start(half_b(a, sign, ds))
-    for a in range(2):
-        for sign in (1, -1):
-            full_b(a, sign, 2).wait_recv()
-            start(half_b(a, sign, 2))
-    pick(1)
-    pick(-1)
+    for db in (1, -1):
+        plan(db)
+        for a in range(2):
+            pick(db, a)
+    for ds in (0, -1, 1, 2):
+        for sign in (1, -1):
+            half_b(2, sign, ds).wait_recv()
+    plan(2)
     for a in range(2):
         for ds in (0, -1, 1, 2):
             for sign in (1, -1):
                 half_b(a, sign, ds).wait_recv()
-    pick(2)
+        pick(2, a)
     for copy in kept:
         copy.wait()
     for slot in range(SIDE):
+        gates_out(slot).wait_recv()
         for a in range(2):
-            b = (place.b + slot) % SIDE
-            to = (1 - place.core) * SIDE + b
-            for r, (first, count) in enumerate(SPANS):
-                remote(
-                    rows.at[slot, a, pl.ds(UNIT + first, count)], outs[a][r].at[to],
-                    out_sem.at[1, slot, a, r], out_sem.at[2, slot, a, r],
-                    place.partner()).wait_recv()
+            for r in range(3):
+                rows_out(slot, a, r).wait_recv()
     for copy in started:
         copy.wait_send()
 
 
-def gather_rows(tokens, cotangent, picks):
+def gather_rows(tokens, cotangent, table):
     width = tokens.shape[1]
     rows_of = tokens.shape[0]
     shapes = [jax.ShapeDtypeStruct((2 * SIDE, count, width), BF) for _, count in SPANS]
+    dma = pltpu.SemaphoreType.DMA
     anywhere = pl.BlockSpec(memory_space=pl.ANY)
     return pl.pallas_call(
         gather_kernel,
-        out_shape=tuple(shapes + shapes),
-        in_specs=[anywhere, anywhere, pl.BlockSpec(memory_space=pltpu.VMEM)],
-        out_specs=(anywhere,) * 6,
+        out_shape=(
+            *shapes, *shapes, jax.ShapeDtypeStruct((2 * SIDE, 8, 256), F32),
+            jax.ShapeDtypeStruct((SIDE, 2, SIDE * rows_of, UNIT), BF),
+        ),
+        in_specs=[anywhere] * 3,
+        out_specs=(anywhere,) * 8,
         scratch_shapes=[
             pltpu.VMEM((2, SIDE, SIDE * rows_of, width), BF),
-            pltpu.VMEM((SIDE, 2, 2 * UNIT, width), BF),
-            pltpu.SemaphoreType.DMA((2,)),
-            pltpu.SemaphoreType.DMA((2, 2, 2, 2, SIDE)),
-            pltpu.SemaphoreType.DMA((2, 2, 2, 2, SIDE)),
-            pltpu.SemaphoreType.DMA((3, SIDE, 2, 3)),
+            pltpu.VMEM((SIDE, SIDE * DEVICES, 128), F32),
+            pltpu.VMEM((SIDE, 2, 2, UNIT, width), BF),
+            pltpu.VMEM((SIDE, 2, UNIT, SIDE * rows_of), BF),
+            pltpu.VMEM((SIDE, 2, SIDE * rows_of, UNIT), BF),
+            pltpu.VMEM((SIDE, 2, 8, 256), F32),
+            dma((3,)),
+            dma((2, 2, 2, 3, SIDE)),
+            dma((2, 2, 2, 3, SIDE)),
+            dma((3, SIDE, 2, 3)),
+            dma((3, SIDE)),
+            dma((SIDE,)),
         ],
         compiler_params=pltpu.CompilerParams(
             collective_id=0, has_side_effects=True, vmem_limit_bytes=60 << 20
         ),
         name="gather_rows",
-    )(tokens, cotangent, picks)
+    )(tokens, cotangent, table)
 
 
 def scatter_kernel(
-    hot_o, cold_o, copy_o, hot_g, cold_g, copy_g, spread_ref, grads_ref,
+    hot_o, cold_o, copy_o, hot_g, cold_g, copy_g, spread_ref, grads_ref, first_ref,
     out_ref, grad_ref, up_ref, down_ref,
-    rows, sums, first_in, second_in, third_in, fourth_in, parts, ring_in, copy_in,
+    rows, sums, first_in, second_in, third_in, fourth_in, parts, ring_in, copy_in, spread,
     in_sem, send_r, recv_r, send_1, recv_1, send_2, recv_2, send_3, recv_3, send_4, recv_4,
-    part_sem, send_z, recv_z, send_c, recv_c,
+    part_sem, send_z, recv_z, send_c, recv_c, spread_sem,
 ):
     place = Place()
     width = out_ref.shape[1]
@@ -481,7 +559,7 @@
             send_z.at[way, spot], recv_z.at[way, spot], place.replica(sign))
 
     def later(sign):
-        return (0, 1, 2) if sign == 1 else (3, 4, 5)
+        return (2, 0, 1) if sign == 1 else (5, 3, 4)
 
     def ring_start():
         for d in (4, 3, 5, 2, 6, 1, 7, 0):
@@ -518,17 +596,21 @@
         if p % 3 == 2:
             add(parts.at[0, p], ring_in.at[0, spot], ring_in.at[1, spot])
             start(hand_over(p // 3))
-            return
+            return None
         total = parts[0, p].astype(F32)
         for way in range(2):
             total = total + ring_in[way, spot].astype(F32)
         if p % 3 == 0:
             hand_over(p // 3).wait_recv()
             total = total + copy_in[p // 3].astype(F32)
-        if p < 3:
-            up_ref[p] = jnp.transpose(total).astype(BF)
-        else:
-            down_ref[p - 3] = total.astype(BF)
+        return total
+
+    def ring_result(i, result):
+        cold = ring_end(3 * i + 1)
+        hot = ring_end(3 * i)
+        hot_first = first_ref[:1, :1] > 0.5
+        for e, value in enumerate((jnp.where(hot_first, hot, cold), jnp.where(hot_first, cold, hot))):
+            result[e] = (jnp.transpose(value) if i == 0 else value).astype(BF)
 
     def unit_copies(slot, a, r):
         first, count = SPANS[r]
@@ -592,8 +674,17 @@
                 start(unit_sends(slot, a, r))
                 unit_copies(slot, a, r).start()
 
+    def spread_copy(slot):
+        b = (place.b + slot) % SIDE
+        turn = order.index(slot) % 2
+        return pltpu.make_async_copy(spread_ref.at[b], spread.at[turn], spread_sem.at[slot])
+
+    for slot in order[:2]:
+        spread_copy(slot).start()
+
     def expand(slot):
-        b = (place.b + slot) % SIDE
+        turn = order.index(slot)
+        spread_copy(slot).wait()
         for a in range(2):
             for r in range(3):
                 unit_copies(slot, a, r).wait()
@@ -602,14 +693,20 @@
             @pl.loop(0, width // 512)
             def _(j):
                 cols = pl.ds(pl.multiple_of(j * 512, 512), 512)
-                sums[slot, a, :, cols] = jnp.dot(
-                    spread_ref[b], rows[slot, a, :, cols], preferred_element_type=F32
-                ).astype(BF)
+                own = jnp.dot(
+                    spread[turn % 2, 0], rows[slot, a, pl.ds(0, UNIT), cols],
+                    preferred_element_type=F32)
+                other = jnp.dot(
+                    spread[turn % 2, 1], rows[slot, a, pl.ds(UNIT, UNIT), cols],
+                    preferred_element_type=F32)
+                sums[slot, a, :, cols] = (own + other).astype(BF)
 
             for sign in (1, -1):
                 start(far(slot, a, sign))
             for sign in (1, -1):
                 start(near(slot, a, sign, (1 + sign) // 2))
+        if turn < 2:
+            spread_copy(order[turn + 2]).start()
 
     def pass_on(slot):
         for a in range(2):
@@ -667,13 +764,13 @@
         result[...] = (
             own[...].astype(F32) + fourth_in[a, 0].astype(F32) + fourth_in[a, 1].astype(F32)
         ).astype(BF)
-    for p in (4, 1, 3, 0):
-        ring_end(p)
+    ring_result(1, down_ref)
+    ring_result(0, up_ref)
     for copy in started:
         copy.wait_send()
 
 
-def scatter_rows(out_rows, grad_rows, spread, grads, rows_of):
+def scatter_rows(out_rows, grad_rows, spread, grads, hot_first, rows_of):
     width = out_rows[0].shape[-1]
     hidden = grads.shape[1]
     piece = width // REPLICAS
@@ -688,7 +785,7 @@
             shape, shape, jax.ShapeDtypeStruct((2, piece, hidden), BF),
             jax.ShapeDtypeStruct((2, hidden, piece), BF),
         ),
-        in_specs=[anywhere] * 6 + [vmem, anywhere],
+        in_specs=[anywhere] * 8 + [vmem],
         out_specs=(vmem,) * 4,
         scratch_shapes=[
             pltpu.VMEM((SIDE, 2, 2 * UNIT, width), BF),
@@ -700,6 +797,7 @@
             pltpu.VMEM((REPLICAS, 6, hidden, piece), BF),
             pltpu.VMEM((2, 21, hidden, piece), BF),
             pltpu.VMEM((2, hidden, piece), BF),
+            pltpu.VMEM((2, 2, SIDE * rows_of, UNIT), BF),
             dma((SIDE, 2, 3)),
             dma((SIDE, 2, 3)),
             dma((SIDE, 2, 3)),
@@ -716,21 +814,13 @@
             dma((2, 21)),
             dma((2,)),
             dma((2,)),
+            dma((SIDE,)),
         ],
         compiler_params=pltpu.CompilerParams(
             collective_id=1, has_side_effects=True, vmem_limit_bytes=67043328
         ),
         name="scatter_rows",
-    )(*out_rows, *grad_rows, spread, grads)
-
-
-def regions(values, fill):
-    lead = values.shape[:-2]
-    hot = values[..., :HOT].reshape(*lead, HOT_U)
-    cold = values[..., HOT : HOT + COLD].reshape(*lead, COLD_U)
-    copied = values[..., HOT + COLD : HOT + COLD + COPY].reshape(*lead, SIDE * COPY)
-    pad = [(0, 0)] * len(lead) + [(0, COPY_U - SIDE * COPY)]
-    return hot, cold, jnp.pad(copied, pad, constant_values=fill)
+    )(*out_rows, *grad_rows, spread, grads, hot_first)
 
 
 def local(
@@ -745,62 +835,23 @@
     copy_up,
     copy_down,
 ):
-    devices = lax.axis_size("expert")
     me = lax.axis_index("expert")
-    core = me % 2
     rows_of, width = tokens.shape
     table, dest, slot = route(expert_ids.T, copy_pick.T, gate_weights.T, copy_expert)
-    sent = jnp.broadcast_to(
-        table.reshape(devices // 2, 1, 2, 128), (devices // 2, 2, 2, 128)
-    ).reshape(devices, 2, 128)
-    tables = lax.all_to_all(sent, "expert", split_axis=0, concat_axis=0, tiled=True)
-    grid = tables.reshape(SIDE, SIDE, 2, 2, 128)
-    by_unit = jnp.stack([grid[:, :, 0], jnp.swapaxes(grid[:, :, 1], 0, 1)])
-    mine = jnp.where(core == 0, by_unit[:, :, :, 0], by_unit[:, :, :, 1])
-    gates = regions(mine[..., 64 : 64 + SLOTS], 0.0)
-    named = jnp.where(core == 0, by_unit[0], by_unit[1])[..., :SLOTS].astype(jnp.int32)
-    named = jnp.where(core == 0, named, named[:, :, ::-1])
-    place = jnp.arange(SIDE, dtype=jnp.int32)[None, :, None, None] * rows_of
-    named = jnp.where(named > 0, place + named - 1, -1)
-    named = jnp.concatenate(regions(jnp.moveaxis(named, 2, 1), -1), axis=-1)
-    named = named.reshape(SIDE, 2 * UNIT)
-    sites = jnp.arange(SIDE * rows_of, dtype=jnp.int32)
-    picks = (named[:, :, None] == sites[None, None, :]).astype(BF)
-    spread = (named[:, None, :] == sites[None, :, None]).astype(BF)
-
-    gathered = gather_rows(tokens, cotangent, picks)
-    hot_slot = copy_expert[(me + 1) % devices] % 2
-    gates = jnp.concatenate([gate.reshape(1, -1) for gate in gates], axis=1)
+    *gathered, gates, spread = gather_rows(tokens, cotangent, table)
     *rows, grads, back = serve(
-        hot_slot.reshape(1),
+        copy_expert,
         [part.reshape(-1, width) for part in gathered],
         gates, up_weight, down_weight, copy_up, copy_down,
     )
     rows = [part.reshape(2 * SIDE, -1, width) for part in rows]
-    layer_output, token_grad, up_parts, down_parts = scatter_rows(
-        rows[:3], rows[3:], spread, grads, rows_of
+    hot_first = copy_expert[(me + 1) % DEVICES] % 2 == 0
+    hot_first = jnp.broadcast_to(hot_first.astype(F32), (8, 128))
+    layer_output, token_grad, up_grad, down_grad = scatter_rows(
+        rows[:3], rows[3:], spread, grads, hot_first, rows_of
     )
-
-    hot_back, cold_back, copy_back = jnp.split(
-        back[0], [2 * SIDE * HOT_U, 2 * SIDE * (HOT_U + COLD_U)]
-    )
-    by_slot = jnp.concatenate(
-        [
-            hot_back.reshape(2, SIDE, SIDE, HOT),
-            cold_back.reshape(2, SIDE, SIDE, COLD),
-            copy_back.reshape(2, SIDE, COPY_U)[:, :, : SIDE * COPY].reshape(2, SIDE, SIDE, COPY),
-        ],
-        axis=-1,
-    )
-    by_source = jnp.stack([by_slot[0], jnp.swapaxes(by_slot[1], 0, 1)], axis=2)
-    by_source = jnp.pad(
-        by_source.reshape(devices, HOT + COLD + COPY), ((0, 0), (0, 128 - HOT - COLD - COPY))
-    )
-    returned = lax.all_to_all(by_source, "expert", split_axis=0, concat_axis=0, tiled=True)
+    returned = lax.all_to_all(back, "expert", split_axis=0, concat_axis=0, tiled=True)
     gate_grad = gate_back(dest, slot, returned).T
-
-    up_grad = jnp.where(hot_slot == 0, up_parts, up_parts[::-1])
-    down_grad = jnp.where(hot_slot == 0, down_parts, down_parts[::-1])
     return layer_output, token_grad, gate_grad, up_grad, down_grad
 
 

time: 287 us -> 261 us (0.909)
  other arithmetic: 7.97 us -> 0 us
  starting transfers between devices: 14.2 us -> 6.32 us
  Pallas kernels: 247 us -> 242 us
  local copies, waits for them, and re-layouts: 10.9 us -> 7.48 us
    all_to_all x2 -> x1, starting transfers between devices: 14.2 us -> 6.32 us  [local(): lax.all_to_all(back, 'expert', split_axis=0, concat_axis=0, tiled=True)]
    pallas_call x1, Pallas kernels: 114 us -> 110 us  [scatter_rows(): pl.pallas_call(scatter_kernel, out_shape=(shape, shape, jax.ShapeDtypeStr...]
    select_n x3 -> x0, other arithmetic: 4.03 us -> none  [the longest x1 2.06 us: local(): down_grad = jnp.where(hot_slot == 0, down_parts, down_parts[::-1])]
    unnamed x6 -> x8, local copies, waits for them, and re-layouts: 2.69 us -> 6.3 us
    convert_element_type x3 -> x0, other arithmetic: 3.08 us -> none  [the longest x1 1.6 us: local(): spread = (named[:, None, :] == sites[None, :, None]).astype(BF)]
  transfers between devices with their start and end apart: 2 -> 1, of which waited for: 1 -> 0; matrix products, arithmetic and copies ran while one was open for 2% -> 0% of each run, Pallas kernels for 40% -> 42%
where the time goes in v1:
time: 261 us; the launch traced here: 259 us
  Pallas kernels  242 us (93%)
  local copies, waits for them, and re-layouts  7.48 us (3%)
  starting transfers between devices  6.32 us (2%)
  between operations  2.67 us (1%)
    pallas_call x1, Pallas kernels, scatter_rows(): pl.pallas_call(scatter_kernel, out_shape=(shape, shape, jax.ShapeDtypeStr...  110 us
    pallas_call x1, Pallas kernels, gather_rows(): pl.pallas_call(gather_kernel, out_shape=(*shapes, *shapes, jax.ShapeDtype...  96.6 us
    pallas_call x1, Pallas kernels, serve(): pl.pallas_call(serve_kernel, out_shape=(*rows, *rows, jax.ShapeDtypeStruc...  30.1 us
    all_to_all x1, starting transfers between devices, local(): lax.all_to_all(back, 'expert', split_axis=0, concat_axis=0, tiled=True)  6.32 us
    unnamed x8, local copies, waits for them, and re-layouts  6.3 us
  transfers between devices with their start and end apart: 1, of which 0 were waited for; matrix products, arithmetic and copies ran while one was open for 0% of the time, Pallas kernels for 42%

profile of v1, /device:TPU:5, one launch (start us, length us, event | category | flops | bytes accessed | tf_op | source)
XLA Modules:
  0.0 258.5 jit_solution(8539774073611613510)
XLA Ops:
  0.6 3.8 %route.1 = (f32[32,128]{1,0:T(8,128)}, s32[8,128]{1,0:T(8,128)}, s32[8,128]{1,0:T(8,128)}) custom-call(s32[8,128]{1,0:T(8,128)} %bitcast.34, s32[8,128]{1,0:T(8,128)} %bitcast.35, f32[8,128]{1,0:T(8,128)} %bitcast.36, s32[32]{0:T(128)} %which_ref.1), custom_call_target="tpu_custom_call" | custom-call | tf_op jit(solution)/shard_map/route/pallas_call | solution.py:66
  4.4 96.6 %gather_rows.1 = (bf16[8,96,2048]{2,1,0:T(8,128)(2,1)}, bf16[8,48,2048]{2,1,0:T(8,128)(2,1)}, bf16[8,32,2048]{2,1,0:T(8,128)(2,1)}, bf16[8,96,2048]{2,1,0:T(8,12...) custom-call(bf16[128,2048]{1,0:T(8,128)(2,1)} %tok_ref.1, ...), custom_call_target="tpu_custom_call" | custom-call | tf_op jit(solution)/shard_map/gather_rows/pallas_call | solution.py:498
  101.1 0.0 copy-start.1
  101.1 30.1 %serve.1 = (bf16[768,2048]{1,0:T(8,128)(2,1)}, bf16[384,2048]{1,0:T(8,128)(2,1)}, bf16[256,2048]{1,0:T(8,128)(2,1)}, bf16[768,2048]{1,0:T(8,128)(2,1)}, bf16[384...) custom-call(s32[32]{0:T(128)} %which_ref.1, ...), custom_call_target="tpu_custom_call" | custom-call | tf_op jit(solution)/shard_map/serve/pallas_call | solution.py:240
  131.1 6.3 %all-to-all-start = ((f32[32,1,128]{2,1,0:T(1,128)}), f32[32,1,128]{2,1,0:T(1,128)}, u32[]{:S(2)}, u32[]{:S(2)}) async-start(f32[32,1,128]{2,1,0:T(1,128)} %bitcast.33), calls=%async_computation | async-start | bytes 32768 | tf_op jit(solution)/shard_map/all_to_all | solution.py:853
  137.5 0.0 copy-done.1
  137.5 0.6 dynamic_slice.3
  140.0 0.6 broadcast_in_dim.3.first_ref
  140.6 109.5 %scatter_rows.1 = (bf16[128,2048]{1,0:T(8,128)(2,1)}, bf16[128,2048]{1,0:T(8,128)(2,1)}, bf16[2,256,384]{2,1,0:T(8,128)(2,1)}, bf16[2,384,256]{2,1,0:T(8,128)(2,1)}) custom-call(bf16[8,96,2048]{2,1,0:T(8,128)(2,1)} %bitcast.21, bf16[8,48,2048]{2,1,0:T(8,128)(2,1)} %bitcast.25, bf16[8,32,2048]{2,1,0:T(8,128)(2,1)} %bitcast.29, bf16[8,96,2048]{2,1,0:T(8,128)(2,1)} %bitcast.22, ...), custom_call_target="tpu_custom_call" | custom-call | tf_op jit(solution)/shard_map/scatter_rows/pallas_call | solution.py:782
  250.2 0.0 copy-start
  250.2 0.0 all-to-all-done
  250.2 2.0 gate_back.1
  252.2 1.9 copy.20
  254.1 1.9 copy.21
  256.0 1.8 copy.22
  257.8 0.0 copy-done
  257.8 0.7 copy.23
Async XLA Ops:
  101.1 36.4 %copy-start.1 = (s32[32]{0:T(128)S(1)}, s32[32]{0:T(128)}, u32[]{:S(2)}) copy-start(s32[32]{0:T(128)} %which_ref.1) | copy-start | bytes 388
  131.1 119.1 %all-to-all-start = ((f32[32,1,128]{2,1,0:T(1,128)}), f32[32,1,128]{2,1,0:T(1,128)}, u32[]{:S(2)}, u32[]{:S(2)}) async-start(f32[32,1,128]{2,1,0:T(1,128)} %bitcast.33), calls=%async_computation | async-start | bytes 32768 | tf_op jit(solution)/shard_map/all_to_all | solution.py:853
  250.2 7.6 %copy-start = (bf16[2,384,256]{2,1,0:T(8,128)(2,1)S(1)}, bf16[2,384,256]{2,1,0:T(8,128)(2,1)}, u32[]{:S(2)}) copy-start(bf16[2,384,256]{2,1,0:T(8,128)(2,1)} %get-tuple-element.60) | copy-start | bytes 1179652

commit v2 on v1

--- a/solution.py
+++ b/solution.py
@@ -24,7 +24,7 @@
     return lax.broadcasted_iota(jnp.int32, shape, dim)
 
 
-def route_kernel(ids_ref, picks_ref, gates_ref, listed_ref, table_ref, dest_ref, slot_ref):
+def route_kernel(ids_ref, picks_ref, gates_ref, listed_ref, table_ref):
     chosen, rows = ids_ref.shape
     ids, picks, gates = ids_ref[...], picks_ref[...], gates_ref[...]
     devices = listed_ref.shape[0]
@@ -47,10 +47,9 @@
         base = jnp.where(region == 0, 0, jnp.where(region == 1, HOT, HOT + COLD))
         slot = base + rank
         to = (dest == iota((devices, rows), 0)).astype(F32)
-        value = jnp.where(slot == lines, token, 0.0) + jnp.where(slot + 64 == lines, g, 0.0)
+        code = token + float(k * rows)
+        value = jnp.where(slot == lines, code, 0.0) + jnp.where(slot + 64 == lines, g, 0.0)
         table = table + across(to, value, EXACT)
-        dest_ref[k : k + 1] = dest
-        slot_ref[k : k + 1] = slot
     table_ref[...] = table
 
 
@@ -61,17 +60,12 @@
 
 
 def route(ids, picks, gates, listed):
-    chosen, rows = ids.shape
     vmem = pl.BlockSpec(memory_space=pltpu.VMEM)
     return pl.pallas_call(
         route_kernel,
-        out_shape=(
-            jax.ShapeDtypeStruct((listed.shape[0], 128), F32),
-            jax.ShapeDtypeStruct((chosen, rows), jnp.int32),
-            jax.ShapeDtypeStruct((chosen, rows), jnp.int32),
-        ),
+        out_shape=jax.ShapeDtypeStruct((listed.shape[0], 128), F32),
         in_specs=[vmem] * 3 + [pl.BlockSpec(memory_space=pltpu.SMEM)],
-        out_specs=(vmem,) * 3,
+        out_specs=vmem,
         name="route",
     )(ids, picks, gates, listed)
 
@@ -85,26 +79,31 @@
     return (hot | cold | copied).astype(F32)
 
 
-def gate_kernel(dest_ref, slot_ref, back_ref, out_ref):
-    chosen, rows = dest_ref.shape
-    devices = back_ref.shape[0]
-    back = jnp.transpose(back_ref[...])
-    for k in range(chosen):
-        to = (dest_ref[k : k + 1] == iota((devices, rows), 0)).astype(F32)
-        picked = jnp.dot(back, to, precision=EXACT, preferred_element_type=F32)
-        mine = jnp.where(slot_ref[k : k + 1] == iota((128, rows), 0), picked, 0.0)
-        out_ref[k : k + 1] = jnp.sum(mine, axis=0, keepdims=True)
-
-
-def gate_back(dest, slot, back):
-    vmem = pl.BlockSpec(memory_space=pltpu.VMEM)
+def finish_kernel(count, *refs):
+    ins, outs, held, sems = refs[:count], refs[count : 2 * count], refs[2 * count : -1], refs[-1]
+    loads = [pltpu.make_async_copy(ins[i], held[i], sems.at[0, i]) for i in range(count)]
+    stores = [pltpu.make_async_copy(held[i], outs[i], sems.at[1, i]) for i in range(count)]
+    for load in loads:
+        load.start()
+    for load, store in zip(loads, stores):
+        load.wait()
+        store.start()
+    for store in stores:
+        store.wait()
+
+
+def finish(*arrays):
+    anywhere = pl.BlockSpec(memory_space=pl.ANY)
+    count = len(arrays)
     return pl.pallas_call(
-        gate_kernel,
-        out_shape=jax.ShapeDtypeStruct(dest.shape, F32),
-        in_specs=[vmem] * 3,
-        out_specs=vmem,
-        name="gate_back",
-    )(dest, slot, back)
+        functools.partial(finish_kernel, count),
+        out_shape=tuple(jax.ShapeDtypeStruct(x.shape, x.dtype) for x in arrays),
+        in_specs=[anywhere] * count,
+        out_specs=(anywhere,) * count,
+        scratch_shapes=[pltpu.VMEM(x.shape, x.dtype) for x in arrays]
+        + [pltpu.SemaphoreType.DMA((2, count))],
+        name="finish",
+    )(*arrays)
 
 
 def serve_kernel(
@@ -115,7 +114,7 @@
     firsts = (0, hot_t.shape[0], hot_t.shape[0] + cold_t.shape[0])
     counts = (hot_t.shape[0], cold_t.shape[0], copy_t.shape[0])
     width = x.shape[1]
-    step = 512
+    step = 1024
     me = lax.axis_index("expert")
     hot = which_ref[(me + 1) % DEVICES] % 2
     ups = (up_ref.at[hot], up_ref.at[1 - hot], copy_up_ref.at[0])
@@ -153,7 +152,7 @@
         gate = gate_cols[span][:, :1]
         ready[0].wait()
         ready[1].wait()
-        tile = min(count, 384)
+        tile = count
 
         @pl.loop(0, count // tile)
         def _(i):
@@ -217,15 +216,8 @@
         store(w.at[r], grads_ref.at[r], r, 2)
         store(w.at[3 + r], grads_ref.at[3 + r], r, 3)
     turned = jnp.transpose(by_unit[...])
-    for s in range(SIDE):
-        lines = jnp.dot(
-            turned, seats(s, by_unit.shape[0], 0), precision=EXACT, preferred_element_type=F32
-        )
-        for b in range(SIDE):
-            for core in range(2):
-                source = ((b * SIDE + s) if core == 0 else (s * SIDE + b)) * 2 + core
-                i = core * SIDE + b
-                back_ref[source : source + 1] = lines[i : i + 1]
+    for i in range(2 * SIDE):
+        back_ref[i] = jnp.broadcast_to(turned[i : i + 1], back_ref.shape[1:])
     for copy in stores:
         copy.wait()
 
@@ -241,7 +233,7 @@
         serve_kernel,
         out_shape=(
             *rows, *rows, jax.ShapeDtypeStruct((6, hidden, width), BF),
-            jax.ShapeDtypeStruct((DEVICES, 128), F32),
+            jax.ShapeDtypeStruct((2 * SIDE, 8, 256), F32),
         ),
         in_specs=[pl.BlockSpec(memory_space=pltpu.SMEM)] + [anywhere] * 6 + [vmem] + [anywhere] * 4,
         out_specs=(anywhere,) * 7 + (vmem,),
@@ -318,8 +310,8 @@
 
 
 def gather_kernel(
-    tok_ref, cot_ref, table_ref, hot_t, cold_t, copy_t, hot_c, cold_c, copy_c, gates_ref, spread_ref,
-    held, tables, rows, picks, spread, gates, own_sem, send, recv, out_sem, gate_sem, spread_sem,
+    tok_ref, cot_ref, table_ref, hot_t, cold_t, copy_t, hot_c, cold_c, copy_c, gates_ref, spread_ref, kinds_ref,
+    held, tables, rows, picks, spread, gates, kinds, own_sem, send, recv, out_sem, gate_sem, spread_sem,
 ):
     place = Place()
     rows_of = tok_ref.shape[0]
@@ -375,22 +367,27 @@
         for h in range(2):
             target = place.me + h * (1 - 2 * place.core)
             scale = jnp.zeros((8, UNIT), F32)
+            kind = jnp.zeros((8, UNIT), F32)
             for s in range(SIDE):
                 line = tables[b, pl.ds(s * DEVICES + target, 1), :]
                 wide = jnp.broadcast_to(line, (128, 128))
-                site = iota((128, 128), 1).astype(F32) + 1.0
-                one = (jnp.transpose(wide) == site).astype(BF)
-                turned = (wide == iota((128, 128), 0).astype(F32) + 1.0).astype(BF)
+                code = wide.astype(jnp.int32) - 1
+                token = jnp.where(code >= 0, code % 128, -1)
+                one = (jnp.transpose(token.astype(F32)) == iota((128, 128), 1).astype(F32)).astype(BF)
+                turned = (token == iota((128, 128), 0)).astype(BF)
                 seat = seats(s, UNIT, 0).astype(BF)
                 span = pl.ds(s * rows_of, rows_of)
                 picks[slot, h, :, span] = jnp.dot(seat, one, preferred_element_type=F32).astype(BF)
                 spread[slot, h, span, :] = across(turned, seat).astype(BF)
                 scale = scale + across(wide[:8], seats(s, UNIT, 64), EXACT)
+                kind = kind + across((code[:8] // 128).astype(F32).astype(BF), seat)
             gates[slot, h, :, pl.ds(0, UNIT)] = scale
+            kinds[slot, h, :, pl.ds(0, UNIT)] = kind
         unit = place.core * SIDE + b
         keep(pltpu.make_async_copy(gates.at[slot, 0], gates_ref.at[unit], gate_sem.at[0, slot]))
         start(gates_out(slot))
-        keep(pltpu.make_async_copy(spread.at[slot], spread_ref.at[b], spread_sem.at[slot]))
+        keep(pltpu.make_async_copy(spread.at[slot], spread_ref.at[b], spread_sem.at[0, slot]))
+        keep(pltpu.make_async_copy(kinds.at[slot], kinds_ref.at[b], spread_sem.at[1, slot]))
 
     def gates_out(slot):
         b = (place.b + slot) % SIDE
@@ -432,6 +429,8 @@
         copy.start()
         kept.append(copy)
 
+    gates[...] = jnp.zeros_like(gates)
+    kinds[...] = jnp.zeros_like(kinds)
     arrays = (2, 0, 1)
     for a in arrays:
         for sign in (1, -1):
@@ -500,9 +499,10 @@
         out_shape=(
             *shapes, *shapes, jax.ShapeDtypeStruct((2 * SIDE, 8, 256), F32),
             jax.ShapeDtypeStruct((SIDE, 2, SIDE * rows_of, UNIT), BF),
+            jax.ShapeDtypeStruct((SIDE, 2, 8, 256), F32),
         ),
         in_specs=[anywhere] * 3,
-        out_specs=(anywhere,) * 8,
+        out_specs=(anywhere,) * 9,
         scratch_shapes=[
             pltpu.VMEM((2, SIDE, SIDE * rows_of, width), BF),
             pltpu.VMEM((SIDE, SIDE * DEVICES, 128), F32),
@@ -510,12 +510,13 @@
             pltpu.VMEM((SIDE, 2, UNIT, SIDE * rows_of), BF),
             pltpu.VMEM((SIDE, 2, SIDE * rows_of, UNIT), BF),
             pltpu.VMEM((SIDE, 2, 8, 256), F32),
+            pltpu.VMEM((SIDE, 2, 8, 256), F32),
             dma((3,)),
             dma((2, 2, 2, 3, SIDE)),
             dma((2, 2, 2, 3, SIDE)),
             dma((3, SIDE, 2, 3)),
             dma((3, SIDE)),
-            dma((SIDE,)),
+            dma((2, SIDE)),
         ],
         compiler_params=pltpu.CompilerParams(
             collective_id=0, has_side_effects=True, vmem_limit_bytes=60 << 20
@@ -525,16 +526,17 @@
 
 
 def scatter_kernel(
-    hot_o, cold_o, copy_o, hot_g, cold_g, copy_g, spread_ref, grads_ref, first_ref,
-    out_ref, grad_ref, up_ref, down_ref,
-    rows, sums, first_in, second_in, third_in, fourth_in, parts, ring_in, copy_in, spread,
+    hot_o, cold_o, copy_o, hot_g, cold_g, copy_g, spread_ref, grads_ref, back_ref, kinds_ref, first_ref,
+    out_ref, grad_ref, gate_ref, up_ref, down_ref,
+    rows, sums, first_in, second_in, third_in, fourth_in,
+    backs, kinds, gate_sums, gate_first, gate_second, gate_third, gate_fourth, parts, ring_in, copy_in, spread,
     in_sem, send_r, recv_r, send_1, recv_1, send_2, recv_2, send_3, recv_3, send_4, recv_4,
-    part_sem, send_z, recv_z, send_c, recv_c, spread_sem,
+    part_sem, send_z, recv_z, send_c, recv_c, spread_sem, back_sem,
 ):
     place = Place()
     width = out_ref.shape[1]
     rows_of = out_ref.shape[0]
-    half = rows_of // 2
+    arrays = (2, 0, 1)
     ins = ((hot_o, cold_o, copy_o), (hot_g, cold_g, copy_g))
     order = (2, 3, 1, 0)
     started = []
@@ -629,46 +631,84 @@
 
     def chunk(slot, a, ds, part=None):
         s = (place.s + ds + SIDE) % SIDE
-        first = pl.multiple_of(s * rows_of, rows_of)
+        count = 16 if a == 2 else rows_of
+        within = gate_sums.at[slot] if a == 2 else sums.at[slot, a]
+        first = pl.multiple_of(s * count, count)
         if part is None:
-            return sums.at[slot, a, pl.ds(first, rows_of)]
-        return sums.at[slot, a, pl.ds(pl.multiple_of(first + part * half, half), half)]
+            return within.at[pl.ds(first, count)]
+        half = count // 2
+        return within.at[pl.ds(pl.multiple_of(first + part * half, half), half)]
+
+    def half_of(within, part):
+        half = within.shape[0] // 2
+        return within.at[pl.ds(part * half, half)]
+
+    def first_at(slot, a, part):
+        return gate_first.at[slot, part] if a == 2 else first_in.at[slot, a, part]
+
+    def second_at(slot, a, way):
+        return gate_second.at[slot, way] if a == 2 else second_in.at[slot, a, way]
+
+    def third_at(a, part):
+        return gate_third.at[part] if a == 2 else third_in.at[a, part]
+
+    def fourth_at(a, way):
+        return gate_fourth.at[way] if a == 2 else fourth_in.at[a, way]
 
     def far(slot, a, sign):
         part = (1 - sign) // 2
         return remote(
-            chunk(slot, a, 2, part), first_in.at[slot, a, part],
+            chunk(slot, a, 2, part), first_at(slot, a, part),
             send_1.at[slot, a, part], recv_1.at[slot, a, part], place.at(0, sign))
 
     def near(slot, a, sign, part):
         way = (1 - sign) // 2
         return remote(
-            chunk(slot, a, sign, part), second_in.at[slot, a, way, pl.ds(part * half, half)],
+            chunk(slot, a, sign, part), half_of(second_at(slot, a, way), part),
             send_2.at[slot, a, way, part], recv_2.at[slot, a, way, part],
             place.at(0, sign))
 
     def far_b(a, sign):
         part = (1 - sign) // 2
         return remote(
-            chunk(2, a, 0, part), third_in.at[a, part],
+            chunk(2, a, 0, part), third_at(a, part),
             send_3.at[a, part], recv_3.at[a, part], place.at(sign, 0))
 
     def near_b(a, sign, part):
         way = (1 - sign) // 2
         return remote(
-            chunk(sign % SIDE, a, 0, part), fourth_in.at[a, way, pl.ds(part * half, half)],
+            chunk(sign % SIDE, a, 0, part), half_of(fourth_at(a, way), part),
             send_4.at[a, way, part], recv_4.at[a, way, part], place.at(sign, 0))
 
     def add(into, *others):
-        @pl.loop(0, into.shape[0] // 32)
+        step = min(32, into.shape[0])
+
+        @pl.loop(0, into.shape[0] // step)
         def _(i):
-            span = pl.ds(pl.multiple_of(i * 32, 32), 32)
+            span = pl.ds(pl.multiple_of(i * step, step), step)
             total = into[span].astype(F32)
             for other in others:
                 total = total + other[span].astype(F32)
-            into[span] = total.astype(BF)
+            into[span] = total.astype(into.dtype)
+
+    def back_copies(slot):
+        b = (place.b + slot) % SIDE
+        return (
+            pltpu.make_async_copy(
+                back_ref.at[place.core * SIDE + b], backs.at[slot, 0], back_sem.at[0, slot]),
+            pltpu.make_async_copy(kinds_ref.at[b], kinds.at[slot], back_sem.at[1, slot]),
+        )
+
+    def back_send(slot):
+        b = (place.s + slot) % SIDE
+        return remote(
+            back_ref.at[(1 - place.core) * SIDE + b], backs.at[slot, 1],
+            back_sem.at[2, slot], back_sem.at[3, slot], place.partner())
 
     for slot in order:
+        start(back_send(slot))
+        for copy in back_copies(slot):
+            copy.start()
         for a in range(2):
             for r in range(3):
                 start(unit_sends(slot, a, r))
@@ -685,6 +725,25 @@
     def expand(slot):
         turn = order.index(slot)
         spread_copy(slot).wait()
+        for copy in back_copies(slot):
+            copy.wait()
+        back_send(slot).wait_recv()
+        gate = jnp.zeros((8, SIDE * rows_of), F32)
+        for h in range(2):
+            kind = kinds[slot, h, :, pl.ds(0, UNIT)]
+            rest = backs[slot, h, :, pl.ds(0, UNIT)]
+            rest = jnp.where(kind == iota((8, UNIT), 0).astype(F32), rest, 0.0)
+            for _ in range(3):
+                top = rest.astype(BF)
+                rest = rest - top.astype(F32)
+                gate = gate + across(top, spread[turn % 2, h])
+        for s in range(SIDE):
+            gate_sums[slot, pl.ds(16 * s, 8)] = gate[:, s * rows_of : (s + 1) * rows_of]
+            gate_sums[slot, pl.ds(16 * s + 8, 8)] = jnp.zeros((8, rows_of), F32)
+        for sign in (1, -1):
+            start(far(slot, 2, sign))
+        for sign in (1, -1):
+            start(near(slot, 2, sign, (1 + sign) // 2))
         for a in range(2):
             for r in range(3):
                 unit_copies(slot, a, r).wait()
@@ -709,19 +768,19 @@
             spread_copy(order[turn + 2]).start()
 
     def pass_on(slot):
-        for a in range(2):
+        for a in arrays:
             for sign in (1, -1):
                 part = (1 - sign) // 2
                 far(slot, a, sign).wait_recv()
-                add(chunk(slot, a, sign, part), first_in.at[slot, a, part])
+                add(chunk(slot, a, sign, part), first_at(slot, a, part))
                 start(near(slot, a, sign, part))
 
     def finish(slot):
-        for a in range(2):
+        for a in arrays:
             for sign in (1, -1):
                 for part in range(2):
                     near(slot, a, sign, part).wait_recv()
-            add(chunk(slot, a, 0), second_in.at[slot, a, 0], second_in.at[slot, a, 1])
+            add(chunk(slot, a, 0), second_at(slot, a, 0), second_at(slot, a, 1))
 
     ring_start()
     expand(2)
@@ -732,45 +791,46 @@
     ring_step(2, False)
     pass_on(3)
     finish(2)
-    for a in range(2):
+    for a in arrays:
         for sign in (1, -1):
             start(far_b(a, sign))
     expand(0)
     ring_step(2, True)
     pass_on(1)
     finish(3)
-    for a in range(2):
+    for a in arrays:
         start(near_b(a, -1, 0))
     ring_step(3, False)
     pass_on(0)
     finish(1)
-    for a in range(2):
+    for a in arrays:
         start(near_b(a, 1, 1))
     ring_step(3, True)
-    for a in range(2):
+    for a in arrays:
         for sign in (1, -1):
             part = (1 - sign) // 2
             far_b(a, sign).wait_recv()
-            add(chunk(sign % SIDE, a, 0, part), third_in.at[a, part])
+            add(chunk(sign % SIDE, a, 0, part), third_at(a, part))
             start(near_b(a, sign, part))
     finish(0)
     for p in (5, 2):
         ring_end(p)
-    for a, result in ((0, out_ref), (1, grad_ref)):
+    for a in arrays:
         for sign in (1, -1):
             for part in range(2):
                 near_b(a, sign, part).wait_recv()
-        own = chunk(0, a, 0)
-        result[...] = (
-            own[...].astype(F32) + fourth_in[a, 0].astype(F32) + fourth_in[a, 1].astype(F32)
-        ).astype(BF)
+        add(chunk(0, a, 0), fourth_at(a, 0), fourth_at(a, 1))
+        if a == 2:
+            gate_ref[...] = chunk(0, a, 0, 0)[...]
+        else:
+            (out_ref, grad_ref)[a][...] = chunk(0, a, 0)[...]
     ring_result(1, down_ref)
     ring_result(0, up_ref)
     for copy in started:
         copy.wait_send()
 
 
-def scatter_rows(out_rows, grad_rows, spread, grads, hot_first, rows_of):
+def scatter_rows(out_rows, grad_rows, spread, grads, back, kinds, hot_first, rows_of):
     width = out_rows[0].shape[-1]
     hidden = grads.shape[1]
     piece = width // REPLICAS
@@ -782,11 +842,12 @@
     return pl.pallas_call(
         scatter_kernel,
         out_shape=(
-            shape, shape, jax.ShapeDtypeStruct((2, piece, hidden), BF),
+            shape, shape, jax.ShapeDtypeStruct((8, rows_of), F32),
+            jax.ShapeDtypeStruct((2, piece, hidden), BF),
             jax.ShapeDtypeStruct((2, hidden, piece), BF),
         ),
-        in_specs=[anywhere] * 8 + [vmem],
-        out_specs=(vmem,) * 4,
+        in_specs=[anywhere] * 10 + [vmem],
+        out_specs=(vmem,) * 5,
         scratch_shapes=[
             pltpu.VMEM((SIDE, 2, 2 * UNIT, width), BF),
             pltpu.VMEM((SIDE, 2, SIDE * rows_of, width), BF),
@@ -794,6 +855,13 @@
             pltpu.VMEM((SIDE, 2, 2, rows_of, width), BF),
             pltpu.VMEM((2, 2, half, width), BF),
             pltpu.VMEM((2, 2, rows_of, width), BF),
+            pltpu.VMEM((SIDE, 2, 8, 256), F32),
+            pltpu.VMEM((SIDE, 2, 8, 256), F32),
+            pltpu.VMEM((SIDE, SIDE * 16, rows_of), F32),
+            pltpu.VMEM((SIDE, 2, 8, rows_of), F32),
+            pltpu.VMEM((SIDE, 2, 16, rows_of), F32),
+            pltpu.VMEM((2, 8, rows_of), F32),
+            pltpu.VMEM((2, 16, rows_of), F32),
             pltpu.VMEM((REPLICAS, 6, hidden, piece), BF),
             pltpu.VMEM((2, 21, hidden, piece), BF),
             pltpu.VMEM((2, hidden, piece), BF),
@@ -801,26 +869,27 @@
             dma((SIDE, 2, 3)),
             dma((SIDE, 2, 3)),
             dma((SIDE, 2, 3)),
-            dma((SIDE, 2, 2)),
-            dma((SIDE, 2, 2)),
-            dma((SIDE, 2, 2, 2)),
-            dma((SIDE, 2, 2, 2)),
-            dma((2, 2)),
-            dma((2, 2)),
-            dma((2, 2, 2)),
-            dma((2, 2, 2)),
+            dma((SIDE, 3, 2)),
+            dma((SIDE, 3, 2)),
+            dma((SIDE, 3, 2, 2)),
+            dma((SIDE, 3, 2, 2)),
+            dma((3, 2)),
+            dma((3, 2)),
+            dma((3, 2, 2)),
+            dma((3, 2, 2)),
             dma((REPLICAS,)),
             dma((2, 21)),
             dma((2, 21)),
             dma((2,)),
             dma((2,)),
             dma((SIDE,)),
+            dma((4, SIDE)),
         ],
         compiler_params=pltpu.CompilerParams(
             collective_id=1, has_side_effects=True, vmem_limit_bytes=67043328
         ),
         name="scatter_rows",
-    )(*out_rows, *grad_rows, spread, grads, hot_first)
+    )(*out_rows, *grad_rows, spread, grads, back, kinds, hot_first)
 
 
 def local(
@@ -837,8 +906,8 @@
 ):
     me = lax.axis_index("expert")
     rows_of, width = tokens.shape
-    table, dest, slot = route(expert_ids.T, copy_pick.T, gate_weights.T, copy_expert)
-    *gathered, gates, spread = gather_rows(tokens, cotangent, table)
+    table = route(expert_ids.T, copy_pick.T, gate_weights.T, copy_expert)
+    *gathered, gates, spread, kinds = gather_rows(tokens, cotangent, table)
     *rows, grads, back = serve(
         copy_expert,
         [part.reshape(-1, width) for part in gathered],
@@ -847,12 +916,11 @@
     rows = [part.reshape(2 * SIDE, -1, width) for part in rows]
     hot_first = copy_expert[(me + 1) % DEVICES] % 2 == 0
     hot_first = jnp.broadcast_to(hot_first.astype(F32), (8, 128))
-    layer_output, token_grad, up_grad, down_grad = scatter_rows(
-        rows[:3], rows[3:], spread, grads, hot_first, rows_of
+    results = scatter_rows(
+        rows[:3], rows[3:], spread, grads, back, kinds, hot_first, rows_of
     )
-    returned = lax.all_to_all(back, "expert", split_axis=0, concat_axis=0, tiled=True)
-    gate_grad = gate_back(dest, slot, returned).T
-    return layer_output, token_grad, gate_grad, up_grad, down_grad
+    layer_output, token_grad, gate_grad, up_grad, down_grad = finish(*results)
+    return layer_output, token_grad, gate_grad.T, up_grad, down_grad
 
 
 def solution(mesh):

time: 261 us -> 247 us (0.946); the launches traced: 259 us -> 247 us
  starting transfers between devices: 6.32 us -> 0 us
  local copies, waits for them, and re-layouts: 7.48 us -> 1.19 us
    all_to_all x1 -> x0, starting transfers between devices: 6.32 us -> none  [local(): lax.all_to_all(back, 'expert', split_axis=0, concat_axis=0, tiled=True)]
    unnamed x8 -> x2, local copies, waits for them, and re-layouts: 6.3 us -> 0.01 us
    pallas_call x1, Pallas kernels: 110 us -> 113 us  [scatter_rows(): pl.pallas_call(scatter_kernel, out_shape=(shape, shape, jax.ShapeDtypeStr...]
    pallas_call x1, Pallas kernels: 30.1 us -> 26.9 us  [serve(): pl.pallas_call(serve_kernel, out_shape=(*rows, *rows, jax.ShapeDtypeStruc...]
  transfers between devices with their start and end apart: 1 -> 0, of which waited for: 0 -> 0; matrix products, arithmetic and copies ran while one was open for 0% -> 0% of each run, Pallas kernels for 42% -> 0%
where the time goes in v2:
time: 247 us
  Pallas kernels  243 us (98%)
  between operations  2.83 us (1%)
    pallas_call x1, Pallas kernels, scatter_rows(): pl.pallas_call(scatter_kernel, out_shape=(shape, shape, jax.ShapeDtypeStr...  113 us
    pallas_call x1, Pallas kernels, gather_rows(): pl.pallas_call(gather_kernel, out_shape=(*shapes, *shapes, jax.ShapeDtype...  96.7 us
    pallas_call x1, Pallas kernels, serve(): pl.pallas_call(serve_kernel, out_shape=(*rows, *rows, jax.ShapeDtypeStruc...  26.9 us

profile of v2, /device:TPU:5, one launch (start us, length us, event | category | flops | bytes accessed | tf_op | source)
XLA Modules:
  0.0 247.1 jit_solution(16784186630521517855)
XLA Ops:
  0.6 3.8 %route.1.table_ref = f32[32,128]{1,0:T(8,128)} custom-call(s32[8,128]{1,0:T(8,128)} %bitcast.29, s32[8,128]{1,0:T(8,128)} %bitcast.30, f32[8,128]{1,0:T(8,128)} %bitcast.31, s32[32]{0:T(128)} %which_ref.1), custom_call_target="tpu_custom_call" | custom-call | tf_op jit(solution)/shard_map/route/pallas_call | solution.py:64
  4.4 96.7 %gather_rows.1 = (bf16[8,96,2048]{2,1,0:T(8,128)(2,1)}, bf16[8,48,2048]{2,1,0:T(8,128)(2,1)}, bf16[8,32,2048]{2,1,0:T(8,128)(2,1)}, bf16[8,96,2048]{2,1,0:T(8,12...) custom-call(bf16[128,2048]{1,0:T(8,128)(2,1)} %tok_ref.1, ...), custom_call_target="tpu_custom_call" | custom-call | tf_op jit(solution)/shard_map/gather_rows/pallas_call | solution.py:497
  101.1 0.0 copy-start
  101.1 26.9 %serve.1 = (bf16[768,2048]{1,0:T(8,128)(2,1)}, bf16[384,2048]{1,0:T(8,128)(2,1)}, bf16[256,2048]{1,0:T(8,128)(2,1)}, bf16[768,2048]{1,0:T(8,128)(2,1)}, bf16[384...) custom-call(s32[32]{0:T(128)} %which_ref.1, ...), custom_call_target="tpu_custom_call" | custom-call | tf_op jit(solution)/shard_map/serve/pallas_call | solution.py:232
  128.1 0.0 copy-done
  128.1 0.6 dynamic_slice.3
  130.6 0.6 broadcast_in_dim.3.first_ref
  131.2 113.4 %scatter_rows.1 = (bf16[128,2048]{1,0:T(8,128)(2,1)}, bf16[128,2048]{1,0:T(8,128)(2,1)}, f32[8,128]{1,0:T(8,128)}, bf16[2,256,384]{2,1,0:T(8,128)(2,1)}, bf16[2,384,256]{2,1,0:T(8,128)(2,1)}) custom-call(bf16[8,96,2048]{2,1,0:T(8,128)(2,1)} %bitcast.17, bf16[8,48,2048]{2,1,0:T(8,128)(2,1)} %bitcast.21, bf16[8,32,2048]{2,1,0:T(8,128)(2,1)} %bitcast.25, ...), custom_call_target="tpu_custom_call" | custom-call | tf_op jit(solution)/shard_map/scatter_rows/pallas_call | solution.py:842
  244.6 2.4 finish.1
Async XLA Ops:
  101.1 27.0 %copy-start = (s32[32]{0:T(128)S(1)}, s32[32]{0:T(128)}, u32[]{:S(2)}) copy-start(s32[32]{0:T(128)} %which_ref.1) | copy-start | bytes 388

commit v3 on v2

--- a/solution.py
+++ b/solution.py
@@ -108,7 +108,7 @@
 
 def serve_kernel(
     which_ref, hot_t, cold_t, copy_t, hot_c, cold_c, copy_c, gates_ref, up_ref, down_ref,
-    copy_up_ref, copy_down_ref, hot_o, cold_o, copy_o, hot_g, cold_g, copy_g, grads_ref, back_ref,
+    copy_up_ref, copy_down_ref, hot_o, cold_o, copy_o, hot_g, cold_g, copy_g, grads_ref, back_ref, first_ref,
     x, c, u, v, o, q, w, linear, slope, active, sums, gate_cols, by_unit, in_sem, out_sem,
 ):
     firsts = (0, hot_t.shape[0], hot_t.shape[0] + cold_t.shape[0])
@@ -117,6 +117,7 @@
     step = 1024
     me = lax.axis_index("expert")
     hot = which_ref[(me + 1) % DEVICES] % 2
+    first_ref[...] = jnp.broadcast_to((1 - hot).astype(F32), first_ref.shape)
     ups = (up_ref.at[hot], up_ref.at[1 - hot], copy_up_ref.at[0])
     downs = (down_ref.at[hot], down_ref.at[1 - hot], copy_down_ref.at[0])
 
@@ -233,10 +234,10 @@
         serve_kernel,
         out_shape=(
             *rows, *rows, jax.ShapeDtypeStruct((6, hidden, width), BF),
-            jax.ShapeDtypeStruct((2 * SIDE, 8, 256), F32),
+            jax.ShapeDtypeStruct((2 * SIDE, 8, 256), F32), jax.ShapeDtypeStruct((8, 128), F32),
         ),
         in_specs=[pl.BlockSpec(memory_space=pltpu.SMEM)] + [anywhere] * 6 + [vmem] + [anywhere] * 4,
-        out_specs=(anywhere,) * 7 + (vmem,),
+        out_specs=(anywhere,) * 7 + (vmem,) * 2,
         scratch_shapes=[
             pltpu.VMEM((total, width), BF),
             pltpu.VMEM((total, width), BF),
@@ -904,18 +905,15 @@
     copy_up,
     copy_down,
 ):
-    me = lax.axis_index("expert")
     rows_of, width = tokens.shape
     table = route(expert_ids.T, copy_pick.T, gate_weights.T, copy_expert)
     *gathered, gates, spread, kinds = gather_rows(tokens, cotangent, table)
-    *rows, grads, back = serve(
+    *rows, grads, back, hot_first = serve(
         copy_expert,
         [part.reshape(-1, width) for part in gathered],
         gates, up_weight, down_weight, copy_up, copy_down,
     )
     rows = [part.reshape(2 * SIDE, -1, width) for part in rows]
-    hot_first = copy_expert[(me + 1) % DEVICES] % 2 == 0
-    hot_first = jnp.broadcast_to(hot_first.astype(F32), (8, 128))
     results = scatter_rows(
         rows[:3], rows[3:], spread, grads, back, kinds, hot_first, rows_of
     )

time: 247 us -> 244 us (0.988)
  no operation moved by 1% of the time
where the time goes in v3:
time: 244 us
  Pallas kernels  243 us (100%)
    pallas_call x1, Pallas kernels, scatter_rows(): pl.pallas_call(scatter_kernel, out_shape=(shape, shape, jax.ShapeDtypeStr...  114 us
    pallas_call x1, Pallas kernels, gather_rows(): pl.pallas_call(gather_kernel, out_shape=(*shapes, *shapes, jax.ShapeDtype...  96.7 us
    pallas_call x1, Pallas kernels, serve(): pl.pallas_call(serve_kernel, out_shape=(*rows, *rows, jax.ShapeDtypeStruc...  26.9 us

profile of v3, /device:TPU:5, one launch (start us, length us, event | category | flops | bytes accessed | tf_op | source)
XLA Modules:
  0.0 244.2 jit_solution(16315862634611854684)
XLA Ops:
  0.6 3.8 %route.1.table_ref = f32[32,128]{1,0:T(8,128)} custom-call(s32[8,128]{1,0:T(8,128)} %bitcast.28, s32[8,128]{1,0:T(8,128)} %bitcast.29, f32[8,128]{1,0:T(8,128)} %bitcast.30, s32[32]{0:T(128)} %which_ref.1), custom_call_target="tpu_custom_call" | custom-call | tf_op jit(solution)/shard_map/route/pallas_call | solution.py:64
  4.4 96.7 %gather_rows.1 = (bf16[8,96,2048]{2,1,0:T(8,128)(2,1)}, bf16[8,48,2048]{2,1,0:T(8,128)(2,1)}, bf16[8,32,2048]{2,1,0:T(8,128)(2,1)}, bf16[8,96,2048]{2,1,0:T(8,12...) custom-call(bf16[128,2048]{1,0:T(8,128)(2,1)} %tok_ref.1, ...), custom_call_target="tpu_custom_call" | custom-call | tf_op jit(solution)/shard_map/gather_rows/pallas_call | solution.py:498
  101.1 26.9 %serve.1 = (bf16[768,2048]{1,0:T(8,128)(2,1)}, bf16[384,2048]{1,0:T(8,128)(2,1)}, bf16[256,2048]{1,0:T(8,128)(2,1)}, bf16[768,2048]{1,0:T(8,128)(2,1)}, bf16[384...) custom-call(s32[32]{0:T(128)} %which_ref.1, ...), custom_call_target="tpu_custom_call" | custom-call | tf_op jit(solution)/shard_map/serve/pallas_call | solution.py:233
  128.0 113.6 %scatter_rows.1 = (bf16[128,2048]{1,0:T(8,128)(2,1)}, bf16[128,2048]{1,0:T(8,128)(2,1)}, f32[8,128]{1,0:T(8,128)}, bf16[2,256,384]{2,1,0:T(8,128)(2,1)}, bf16[2,384,256]{2,1,0:T(8,128)(2,1)}) custom-call(bf16[8,96,2048]{2,1,0:T(8,128)(2,1)} %bitcast.16, bf16[8,48,2048]{2,1,0:T(8,128)(2,1)} %bitcast.20, bf16[8,32,2048]{2,1,0:T(8,128)(2,1)} %bitcast.24, ...), custom_call_target="tpu_custom_call" | custom-call | tf_op jit(solution)/shard_map/scatter_rows/pallas_call | solution.py:843
  241.7 2.4 finish.1
